TPU v7x, 512 devices: a whole 4x4x16 slice. The times are simulated.
512 devices in a mesh: mem: 32 (over x_hi, z), gx: 4 (over x_lo, core), gy: 4 (over y).
Axes of the slice: x: 4 (x_hi: 2, x_lo: 2; x = x_hi * 2 + x_lo), y: 4, z: 16, core: 2. Of those that a mesh axis runs over, the one named last changes fastest.
Arguments:
- control: float32 [64, 1024, 1024], P('mem', 'gx', 'gy'), may hold values from -6 to 6
- ensemble: bfloat16 [64, 1024, 1024], P('mem', 'gx', 'gy'), may hold values from -0.75 to 0.75
- obs_index: int32 [1024, 256], P('gx', 'gy'), may hold values from 0 to 255
- obs_value: float32 [1024, 256], P('gx', 'gy'), may hold values from -12 to 12
- obs_weight: float32 [1024, 256], P('gx', 'gy'), may hold values from 1 to 16
Outputs:
- gradient: float32 [64, 1024, 1024], P('mem', 'gx', 'gy')
Inputs may be any that keep to these rules, and one draw needn't show every extreme that they name: obs_index[r, j] is a column inside the y tile j // 64; several observations may share a cell.
All inputs are finite; a program needn't handle non-finite values.
Results may differ from a plain program's by a relative error of at most 0.0003.
Values sent between devices are 32-bit elements; how exact they have to be, the bound alone decides.
A program may use at most 64 MiB of HBM per device.

v0:
```python
import math

import jax
import jax.numpy as jnp
from jax import lax
from jax.sharding import PartitionSpec as P

LEN = 400


saturation = 1.5
highest = lax.Precision.HIGHEST


def from_behind(value, axis, steps):
    count = lax.axis_size(axis)
    leading, last = (max(0, -steps), min(count, count - steps))
    return lax.ppermute(value, axis, [(source, source + steps) for source in range(leading, last)])


def pair_scale():
    decay_rate = math.exp(-1.0 / LEN)
    return (1.0 - decay_rate * decay_rate) / (1.0 + decay_rate * decay_rate)


def filter_tables(length):
    decay_log = -1.0 / LEN
    unit_gain = math.sqrt(1.0 - math.exp(2.0 * decay_log))
    positions = jnp.arange(length, dtype=jnp.float32)
    offsets = positions[:, None] - positions[None, :]
    forward_matrix = jnp.where(
        offsets >= 0, unit_gain * jnp.exp(jnp.maximum(offsets, 0.0) * decay_log), 0.0
    )
    carry_weights = jnp.exp((positions + 1.0) * decay_log)
    chain_factor = jnp.float32(math.exp(length * decay_log))
    return (forward_matrix, carry_weights, chain_factor)


def sweep_x_forward(grid_field):
    forward_matrix, carry_weights, chain_factor = filter_tables(grid_field.shape[1])
    boundary = jnp.einsum("j,mjc->mc", forward_matrix[-1], grid_field, precision=highest)
    local_part = jnp.einsum("ij,mjc->mic", forward_matrix, grid_field, precision=highest)
    incoming = jnp.zeros_like(boundary)
    for repeat in range(lax.axis_size("gx") - 1):
        incoming = from_behind(chain_factor * incoming + boundary, "gx", 1)
    return local_part + carry_weights[None, :, None] * incoming[:, None, :]


def sweep_x_backward(grid_field):
    forward_matrix, carry_weights, chain_factor = filter_tables(grid_field.shape[1])
    boundary = jnp.einsum("j,mjc->mc", forward_matrix[:, 0], grid_field, precision=highest)
    local_part = jnp.einsum("ji,mjc->mic", forward_matrix, grid_field, precision=highest)
    incoming = jnp.zeros_like(boundary)
    for repeat in range(lax.axis_size("gx") - 1):
        incoming = from_behind(chain_factor * incoming + boundary, "gx", -1)
    return local_part + carry_weights[::-1][None, :, None] * incoming[:, None, :]


def sweep_y_forward(grid_field):
    forward_matrix, carry_weights, chain_factor = filter_tables(grid_field.shape[2])
    boundary = jnp.einsum("mrj,j->mr", grid_field, forward_matrix[-1], precision=highest)
    local_part = jnp.einsum("mrj,ij->mri", grid_field, forward_matrix, precision=highest)
    incoming = jnp.zeros_like(boundary)
    for repeat in range(lax.axis_size("gy") - 1):
        incoming = from_behind(chain_factor * incoming + boundary, "gy", 1)
    return local_part + incoming[:, :, None] * carry_weights[None, None, :]


def sweep_y_backward(grid_field):
    forward_matrix, carry_weights, chain_factor = filter_tables(grid_field.shape[2])
    boundary = jnp.einsum("mrj,j->mr", grid_field, forward_matrix[:, 0], precision=highest)
    local_part = jnp.einsum("mrj,ji->mri", grid_field, forward_matrix, precision=highest)
    incoming = jnp.zeros_like(boundary)
    for repeat in range(lax.axis_size("gy") - 1):
        incoming = from_behind(chain_factor * incoming + boundary, "gy", -1)
    return local_part + incoming[:, :, None] * carry_weights[::-1][None, None, :]


def smooth(grid_field):
    along_x = sweep_x_backward(sweep_x_forward(grid_field))
    return pair_scale() * sweep_y_backward(sweep_y_forward(along_x))


def smooth_adjoint(grid_field):
    along_y = sweep_y_backward(sweep_y_forward(grid_field))
    return pair_scale() * sweep_x_backward(sweep_x_forward(along_y))


def obs_residual(grid_field, columns, values, weights):
    picked = jnp.take_along_axis(grid_field, columns, axis=1)
    misfit = picked - values
    return weights * saturation * jnp.tanh(misfit / saturation)


def place_residual(residual, columns, like_field):
    row_ids = lax.broadcasted_iota(jnp.int32, columns.shape, 0)
    return jnp.zeros_like(like_field).at[row_ids, columns].add(residual)


def on_device(control, ensemble, obs_index, obs_value, obs_weight):
    smoothed = smooth(control)
    partial_value = jnp.sum(ensemble * smoothed, axis=0)
    increment = lax.psum(partial_value, "mem")
    forcing = place_residual(
        obs_residual(increment, obs_index, obs_value, obs_weight), obs_index, increment
    )
    adjoint = smooth_adjoint(ensemble * forcing[None])
    return control + adjoint


def solution(mesh):
    return jax.shard_map(
        on_device,
        mesh=mesh,
        in_specs=(
            P("mem", "gx", "gy"),
            P("mem", "gx", "gy"),
            P("gx", "gy"),
            P("gx", "gy"),
            P("gx", "gy"),
        ),
        out_specs=P("mem", "gx", "gy"),
        check_vma=False,
    )
```

profile of v0, /device:TPU:1, one launch (start us, length us, event | category | flops | bytes accessed | tf_op | source)
XLA Modules:
  0.0 676.7 jit_solution(3496676984004328318)
XLA Ops:
  6.8 1.4 fusion.64
  8.2 4.5 collective-permute-start
  12.7 4.3 collective-permute-done
  17.0 1.9 collective-permute-start.1
  18.9 0.7 convolution_bitcast_fusion.3
  20.1 3.8 collective-permute-start.2
  23.8 0.7 collective-permute-done.2
  24.5 0.5 fusion.7
  25.0 1.9 collective-permute-start.3
  26.9 3.5 collective-permute-done.3
  30.5 1.9 collective-permute-start.4
  32.4 3.0 collective-permute-done.4
  35.4 1.9 collective-permute-start.5
  37.4 2.9 collective-permute-done.5
  40.2 1.1 fusion
  41.7 1.9 collective-permute-start.6
  43.6 0.7 collective-permute-done.6
  44.4 3.6 collective-permute-start.7
  48.0 0.7 collective-permute-done.7
  48.7 3.7 collective-permute-start.8
  52.3 1.0 fusion.15
  53.4 0.6 fusion.8
  54.1 1.3 collective-permute-start.9
  55.4 3.0 collective-permute-done.9
  58.4 1.3 collective-permute-start.10
  59.7 3.0 collective-permute-done.10
  62.7 1.3 collective-permute-start.11
  64.2 2.9 collective-permute-done.11
  67.0 0.9 fusion.4
  67.9 0.8 copy.121
  69.3 289.4 %all-reduce.2.cloned.1.call-done = f32[256,256]{1,0:T(8,128)} async-done(((f32[256,256]{1,0:T(8,128)}), f32[256,256]{1,0:T(8,128)}) %all-reduce.2.cloned.1.call-update) | async-done | bytes 262160 | tf_op jit(solution)/shard_map/psum | solution.py:103
  358.8 109.0 %gather_fusion = f32[16384]{0:T(1024)S(1)} fusion(f32[256,256]{1,0:T(8,128)} %all-reduce.2.cloned.1.call-done, s32[16384]{0:T(1024)S(1)} %reshape.46), kind=kCustom, calls=%fused_computation | custom fusion | bytes 262144 | tf_op jit(solution)/shard_map/jit(take_along_axis)/gather | solution.py:90
  468.2 113.5 %scatter_custom_fusion = f32[65536]{0:T(1024)S(1)} fusion(s32[16384]{0:T(1024)S(1)} %reshape.52, f32[16384]{0:T(1024)S(1)} %reshape.54, f32[]{:T(128)} %constant.12.clone.1), kind=kCustom, calls=%fused_computation.52 | custom fusion | flops 16384 | bytes 262148
  582.0 0.4 fusion.5
  582.4 3.1 collective-permute-start.12
  585.5 0.7 collective-permute-done.12
  586.2 3.6 collective-permute-start.13
  589.8 0.7 collective-permute-done.13
  590.5 3.6 collective-permute-start.14
  594.1 1.0 fusion.6
  595.2 0.6 fusion.9
  595.8 1.3 collective-permute-start.15
  597.1 3.0 collective-permute-done.15
  600.2 1.3 collective-permute-start.16
  601.5 3.0 collective-permute-done.16
  604.5 1.5 collective-permute-start.17
  606.0 2.8 collective-permute-done.17
  608.8 0.8 convolution_add_fusion
  609.6 0.5 fusion.66
  610.1 30.8 %collective-permute-start.18 = (f32[2,256]{1,0:T(2,128)S(1)}, f32[2,256]{1,0:T(2,128)S(1)}, u32[]{:S(2)}, u32[]{:S(2)}) collective-permute-start(f32[2,256]{1,0:T(2,128)S(1)} %bitcast.136), channel_id=1, source_target_pairs={{0,4},{4,8},{8,12},{1,5},{5,9},{9,13},{2,6},{6,10},{10,14},{3,7},{... | collective-permute-start | bytes 6152 | tf_op jit(solution)/shard_map/ppermute | solution.py:18
  641.0 0.7 collective-permute-done.18
  641.7 4.2 collective-permute-start.19
  645.9 0.7 collective-permute-done.19
  646.6 4.2 collective-permute-start.20
  650.8 0.7 collective-permute-done.20
  651.5 0.7 fusion.1
  652.6 1.9 collective-permute-start.21
  654.5 3.5 collective-permute-done.21
  658.1 1.9 collective-permute-start.22
  660.0 3.0 collective-permute-done.22
  663.0 1.9 collective-permute-start.23
  665.1 2.8 collective-permute-done.23
  667.9 1.0 multiply_add_fusion
  668.9 1.0 copy.135
  (66 shorter events, 3.1 us)
Async XLA Ops:
  6.5 12.4 %copy-start = (f32[2,256,256]{2,1,0:T(8,128)S(1)}, f32[2,256,256]{2,1,0:T(8,128)}, u32[]{:S(2)}) copy-start(f32[2,256,256]{2,1,0:T(8,128)} %param.5) | copy-start | bytes 1572868
  6.5 352.2 %all-reduce.2.cloned.1.call-start = ((), (), s32[]{:S(2)}) async-start(), calls=%async_computation | async-start | bytes 524288 | tf_op jit(solution)/shard_map/psum | solution.py:103
  8.2 8.8 %collective-permute-start = (f32[2,256]{1,0:T(2,128)S(1)}, f32[2,256]{1,0:T(2,128)S(1)}, u32[]{:S(2)}, u32[]{:S(2)}) collective-permute-start(f32[2,256]{1,0:T(2,128)S(1)} %bitcast.130), channel_id=1, source_target_pairs={{0,4},{4,8},{8,12},{1,5},{5,9},{9,13},{2,6},{6,10},{10,14},{3,7},{... | collective-permute-start | bytes 6152 | tf_op jit(solution)/shard_map/ppermute | solution.py:18
  17.0 3.0 collective-permute-start.1
  20.1 4.5 collective-permute-start.2
  25.0 5.4 collective-permute-start.3
  30.5 4.9 collective-permute-start.4
  35.4 4.9 collective-permute-start.5
  41.7 2.6 collective-permute-start.6
  44.4 4.3 collective-permute-start.7
  48.7 4.7 collective-permute-start.8
  53.4 6.3 copy-start.1
  53.4 10.6 %copy-start.2 = (bf16[2,256,256]{2,1,0:T(8,128)(2,1)S(1)}, bf16[2,256,256]{2,1,0:T(8,128)(2,1)}, u32[]{:S(2)}) copy-start(bf16[2,256,256]{2,1,0:T(8,128)(2,1)} %param.6) | copy-start | bytes 786436
  54.1 4.3 collective-permute-start.9
  58.4 4.3 collective-permute-start.10
  62.7 4.3 collective-permute-start.11
  67.9 0.9 copy-start.5
  69.3 398.6 %copy-start.3 = (f32[256,64]{0,1:T(8,128)S(1)}, f32[256,64]{0,1:T(8,128)}, u32[]{:S(2)}) copy-start(f32[256,64]{0,1:T(8,128)} %param.8) | copy-start | bytes 196612
  69.3 398.6 %copy-start.4 = (f32[256,64]{0,1:T(8,128)S(1)}, f32[256,64]{0,1:T(8,128)}, u32[]{:S(2)}) copy-start(f32[256,64]{0,1:T(8,128)} %param.9) | copy-start | bytes 196612
  582.4 3.8 collective-permute-start.12
  586.2 4.3 collective-permute-start.13
  590.5 4.6 collective-permute-start.14
  595.8 4.3 collective-permute-start.15
  600.2 4.3 collective-permute-start.16
  604.5 4.3 collective-permute-start.17
  610.1 31.6 %collective-permute-start.18 = (f32[2,256]{1,0:T(2,128)S(1)}, f32[2,256]{1,0:T(2,128)S(1)}, u32[]{:S(2)}, u32[]{:S(2)}) collective-permute-start(f32[2,256]{1,0:T(2,128)S(1)} %bitcast.136), channel_id=1, source_target_pairs={{0,4},{4,8},{8,12},{1,5},{5,9},{9,13},{2,6},{6,10},{10,14},{3,7},{... | collective-permute-start | bytes 6152 | tf_op jit(solution)/shard_map/ppermute | solution.py:18
  641.7 4.9 collective-permute-start.19
  646.6 4.9 collective-permute-start.20
  652.6 5.4 collective-permute-start.21
  658.1 4.9 collective-permute-start.22
  663.0 4.9 collective-permute-start.23
Sparse Core Ops, SparseCore 0:
  68.9 289.8 all-reduce.1
where the time goes:
time: 677 us
  waiting for transfers between devices  336 us (50%)
  other arithmetic  114 us (17%)
  local copies, waits for them, and re-layouts  112 us (17%)
  starting transfers between devices  88.2 us (13%)
  between operations  13.9 us (2%)
  matrix products  12.1 us (2%)
    psum x1, waiting for transfers between devices, on_device(): increment = lax.psum(partial_value, 'mem')  289 us
    unnamed x4, other arithmetic  114 us
    gather x3, local copies, waits for them, and re-layouts, obs_residual(): picked = jnp.take_along_axis(grid_field, columns, axis=1)  109 us
    ppermute x24, starting transfers between devices, from_behind(): lax.ppermute(value, axis, [(source, source + steps) for source in range(l...  88.2 us
    ppermute x24, waiting for transfers between devices, from_behind(): lax.ppermute(value, axis, [(source, source + steps) for source in range(l...  46.8 us
  transfers between devices with their start and end apart: 25, of which 23 were waited for; matrix products, arithmetic and copies ran while one was open for 1% of the time, Pallas kernels for 0%

commit v1 on v0

v1 whole, which is shorter than its diff:
```python
import functools
import math

import jax
import jax.numpy as jnp
from jax import lax
from jax.experimental import pallas as pl
from jax.experimental.pallas import tpu as pltpu
from jax.sharding import PartitionSpec as P

LEN = 400
TILE = 256
GRID = 4
RING = 16
NX = GRID * TILE
OBS = 64
saturation = 1.5
MESH = pl.DeviceIdType.MESH
f32 = jnp.float32
bf16 = jnp.bfloat16
i32 = jnp.int32
FAR = 1 << 20

PLANE = [(dx, dy) for dy in (2, 1, 3, 0) for dx in (2, 3, 1, 0) if (dx, dy) != (0, 0)]
GATHER = [(dz, dx) for dz in (2, 1, -1, 0) for dx in (1, 0) if (dz, dx) != (0, 0)]
SPREAD = [(-dz, dx) for dz, dx in GATHER]
ACROSS = [(8, 0), (4, 0), (-4, 0)]


def pair_scale():
    decay_rate = math.exp(-1.0 / LEN)
    return (1.0 - decay_rate * decay_rate) / (1.0 + decay_rate * decay_rate)


def decay(steps):
    return jnp.exp(steps.astype(f32) * (-1.0 / LEN))


def split(x):
    high = x.astype(bf16)
    return high, (x - high.astype(f32)).astype(bf16)


def dot(a, b, left=1, right=0):
    return lax.dot_general(a, b, (((left,), (right,)), ((), ())), preferred_element_type=f32)


def take(x, lanes):
    return jnp.take_along_axis(x, lanes, axis=1)


def iota(shape, dim):
    return lax.broadcasted_iota(i32, shape, dim)


def in_plane(dx, dy):
    return {
        "gx": lax.rem(lax.axis_index("gx") + dx, GRID),
        "gy": lax.rem(lax.axis_index("gy") + dy, GRID),
    }


def in_mem(dz, dx):
    mem = lax.axis_index("mem")
    z, half = lax.rem(mem, RING), mem // RING
    return {"mem": lax.rem(half + dx, 2) * RING + lax.rem(z + dz + RING, RING)}


def piece_of(dz, dx):
    mem = lax.axis_index("mem")
    z, half = lax.rem(mem, RING), mem // RING
    return lax.rem(z + dz + RING, 4) * 2 + lax.rem(half + dx, 2)


def coefficients(axis, d, even, shape):
    me = lax.axis_index(axis)
    it = lax.rem(me - d + GRID, GRID)
    before = jnp.where(it < me, TILE * (me - it - 1) + 1, FAR)
    after = jnp.where(it > me, TILE * (it - me - 1) + 1, FAR)
    ends = 2 * NX - TILE * (me + it + 2) + 2
    own = decay(jnp.where(even, before, after))
    above = jnp.where(even, 0.0, -decay(jnp.full(shape, ends, i32)))
    return own, above


def kernel(
    control, ensemble, obs_index, obs_value, obs_weight, out,
    ctl, ens, idx, val, wgt, thi, tlo, vhi, vlo, w0, part, idxp, first,
    msg, rx, ry, rg, pkb, gat, mid, acr, resb,
    load_sem, plane_send, plane_recv, gs, gr, xs, xr, ss, sr,
):
    own = piece_of(0, 0)
    loads = [
        pltpu.make_async_copy(control, ctl, load_sem.at[0]),
        pltpu.make_async_copy(obs_index, idx, load_sem.at[1]),
        pltpu.make_async_copy(ensemble, ens, load_sem.at[2]),
    ]
    for half in range(2):
        rows = pl.ds(pl.multiple_of(half * 128 + own * 16, 16), 16)
        loads.append(pltpu.make_async_copy(obs_value.at[rows], val.at[half], load_sem.at[3 + half]))
        loads.append(pltpu.make_async_copy(obs_weight.at[rows], wgt.at[half], load_sem.at[5 + half]))
    for copy in loads:
        copy.start()

    barrier = pltpu.get_barrier_semaphore()
    peers = [in_plane(*o) for o in PLANE]
    peers += [in_mem(*o) for o in sorted(set(GATHER + SPREAD + ACROSS))]
    for peer in peers:
        pl.semaphore_signal(barrier, 1, device_id=peer, device_id_type=MESH)

    square = (TILE, TILE)
    table = decay(jnp.abs(iota(square, 0) - iota(square, 1)))
    high, low = split(table)
    thi[...] = high
    tlo[...] = low
    wide = (8, TILE)
    row, column = iota(wide, 0), iota(wide, 1)
    even = (row & 1) == 0
    ends = decay(jnp.where(even, TILE - 1 - column, column))
    starts = decay(jnp.where(even, column, TILE - 1 - column))
    f_row, b_row = ends[0:1], ends[1:2]
    ends_hi = ends.astype(bf16).astype(f32)
    ends16 = jnp.concatenate([ends_hi, ends - ends_hi], axis=0).astype(bf16)
    narrow = (8, 128)
    left = iota(narrow, 1) < 64
    cx = [coefficients("gx", d, even, wide) for d in range(GRID)]
    cy = [coefficients("gy", d, even, wide) for d in range(GRID)]
    cl = [coefficients("gy", d, left, narrow) for d in range(GRID)]
    lane16 = iota((16, 128), 1)
    left16 = lane16 < 64

    def fold(x):
        return x[0:8] + x[8:16]

    sends = []

    def begin(turn):
        sums = []
        for side in range(2):
            for m in range(2):
                sums.append(fold(dot(ends16, vhi[m], 1, side) + dot(ends16, vlo[m], 1, side)))
        x = jnp.where(row < 2, sums[0], jnp.where(row < 4, sums[1], jnp.where(row < 6, sums[2], sums[3])))
        x_hi = x.astype(bf16).astype(f32)
        x16 = jnp.concatenate([x_hi, x - x_hi], axis=0).astype(bf16)
        corner_f = jnp.sum(x * f_row, axis=1, keepdims=True)
        corner_b = jnp.sum(x * b_row, axis=1, keepdims=True)
        msg[turn, :, 0:TILE] = fold(dot(x16, thi[...]) + dot(x16, tlo[...]))
        msg[turn, :, TILE:] = jnp.where(left, corner_f, corner_b)
        copies = []
        for n, (dx, dy) in enumerate(PLANE):
            if dy == 0:
                src, dst = msg.at[turn], rx.at[turn, dx]
            elif dx == 0:
                src, dst = msg.at[turn], ry.at[turn, dy]
            else:
                src, dst = msg.at[turn, :, pl.ds(TILE, 128)], rg.at[turn, n]
            copy = pltpu.make_async_remote_copy(
                src, dst, plane_send.at[turn, n], plane_recv.at[turn, n],
                device_id=in_plane(dx, dy), device_id_type=MESH,
            )
            copy.start()
            copies.append(copy)
        sends.extend(copies)
        for m in range(2):
            u = dot(thi[...], vhi[m]) + dot(tlo[...], vhi[m]) + dot(thi[...], vlo[m])
            uhi, ulo = split(u)
            w0[m] = dot(uhi, thi[...]) + dot(ulo, thi[...]) + dot(uhi, tlo[...])
        return copies

    def finish(turn, copies):
        for copy in copies:
            copy.wait_recv()
        xs_, ys_ = 0.0, 0.0
        for d in range(GRID):
            a = msg[turn, :, 0:TILE] if d == 0 else rx[turn, d, :, 0:TILE]
            xs_ = xs_ + cx[d][0] * a + cx[d][1] * pltpu.roll(a, 1, 0)
            a = msg[turn, :, 0:TILE] if d == 0 else ry[turn, d, :, 0:TILE]
            ys_ = ys_ + cy[d][0] * a + cy[d][1] * pltpu.roll(a, 1, 0)
        corner = 0.0
        for dy in range(GRID):
            over_x = 0.0
            for dx in range(GRID):
                if (dx, dy) == (0, 0):
                    g = msg[turn, :, TILE:]
                elif dy == 0:
                    g = rx[turn, dx, :, TILE:]
                elif dx == 0:
                    g = ry[turn, dy, :, TILE:]
                else:
                    g = rg[turn, PLANE.index((dx, dy))]
                over_x = over_x + cx[dx][0][:, 0:128] * g + cx[dx][1][:, 0:128] * pltpu.roll(g, 1, 0)
            corner = corner + cl[dy][0] * over_x + cl[dy][1] * pltpu.roll(over_x, 64, 1)
        ab = jnp.where(row < 4, xs_ + corner[:, 0:1] * b_row + corner[:, 64:65] * f_row, ys_)
        a = jnp.where(row < 4, starts, ab)
        b = jnp.where(row < 4, ab, starts)
        b = jnp.concatenate([jnp.where((row & 2) == 0, b, 0.0), jnp.where((row & 2) == 0, 0.0, b)], axis=1)
        a_hi, b_hi = a.astype(bf16).astype(f32), b.astype(bf16).astype(f32)
        a_lo, b_lo = a - a_hi, b - b_hi
        a = jnp.concatenate([a_hi, a_hi, a_lo, a_lo], axis=0).astype(bf16)
        b = jnp.concatenate([b_hi, b_lo, b_hi, b_lo], axis=0).astype(bf16)
        return dot(a, b, 0, 0)

    loads[0].wait()
    for m in range(2):
        high, low = split(ctl[m])
        vhi[m] = high
        vlo[m] = low
    pl.semaphore_wait(barrier, len(peers))
    copies = begin(0)
    for copy in loads[1:]:
        copy.wait()
    idxp[...] = jnp.concatenate([idx[0:128], idx[128:256]], axis=1)
    update = finish(0, copies)
    part[...] = (
        ens[0].astype(f32) * (w0[0] + update[:, 0:TILE])
        + ens[1].astype(f32) * (w0[1] + update[:, TILE:])
    )

    def pick(k, carry):
        top = pl.ds(pl.multiple_of(k * 16, 16), 16)
        bottom = pl.ds(pl.multiple_of(128 + k * 16, 16), 16)
        at = idxp[top, :]
        low = at & 127
        upper = at >= 128
        above = jnp.where(upper, take(part[top, 128:256], low), take(part[top, 0:128], low))
        below = jnp.where(upper, take(part[bottom, 128:256], low), take(part[bottom, 0:128], low))
        pkb[k] = jnp.where(left16, above, below)
        return carry

    lax.fori_loop(0, 8, pick, 0)

    copies = []
    for n, (dz, dx) in enumerate(GATHER):
        copy = pltpu.make_async_remote_copy(
            pkb.at[piece_of(dz, dx)], gat.at[n], gs.at[n], gr.at[n],
            device_id=in_mem(dz, dx), device_id_type=MESH,
        )
        copy.start()
        copies.append(copy)
    sends.extend(copies)

    at = idxp[pl.ds(pl.multiple_of(own * 16, 16), 16), :]
    link = jnp.full((16, 128), -1, i32)
    for j in range(OBS):
        here = jnp.where(left16, at[:, j : j + 1], at[:, OBS + j : OBS + j + 1])
        where_ = jnp.where(left16, j, OBS + j)
        link = jnp.where((here == at) & (lane16 > where_), where_, link)
    links = []
    for level in range(6):
        links.append(link)
        link = jnp.where(link >= 0, take(link, jnp.maximum(link, 0)), -1)
    value = jnp.concatenate([val[0], val[1]], axis=1)
    weight = jnp.concatenate([wgt[0], wgt[1]], axis=1) * (saturation * pair_scale())

    total = pkb[own]
    for n, copy in enumerate(copies):
        copy.wait_recv()
        total = total + gat[n]
    mid[...] = total
    copies = []
    for n, (dz, dx) in enumerate(ACROSS):
        copy = pltpu.make_async_remote_copy(
            mid, acr.at[n], xs.at[n], xr.at[n], device_id=in_mem(dz, dx), device_id_type=MESH
        )
        copy.start()
        copies.append(copy)
    sends.extend(copies)

    def find(k, carry):
        at = idxp[pl.ds(pl.multiple_of(k * 8, 8), 8), :]
        lane = iota(narrow, 1)
        found = [jnp.full(narrow, -1, i32) for _ in range(4)]
        for j in range(OBS):
            for half in range(2):
                here = jnp.broadcast_to(at[:, half * OBS + j : half * OBS + j + 1], narrow)
                found[half * 2] = jnp.where(here == lane, half * OBS + j, found[half * 2])
                found[half * 2 + 1] = jnp.where(here == lane + 128, half * OBS + j, found[half * 2 + 1])
        for half in range(2):
            rows = pl.ds(pl.multiple_of(half * 128 + k * 8, 8), 8)
            first[rows, 0:128] = found[half * 2]
            first[rows, 128:256] = found[half * 2 + 1]
        return carry

    lax.fori_loop(0, 16, find, 0)

    for n, copy in enumerate(copies):
        copy.wait_recv()
        total = total + acr[n]
    misfit = pair_scale() * total - value
    residual = weight * jnp.tanh(misfit * (1.0 / saturation))
    for link in links:
        residual = residual + jnp.where(link >= 0, take(residual, jnp.maximum(link, 0)), 0.0)
    resb[own] = residual
    copies = []
    for n, (dz, dx) in enumerate(SPREAD):
        copy = pltpu.make_async_remote_copy(
            resb.at[own], resb.at[own], ss.at[n], sr.at[n],
            device_id=in_mem(dz, dx), device_id_type=MESH,
        )
        copy.start()
        copies.append(copy)
    sends.extend(copies)
    for copy in copies:
        copy.wait_recv()

    def place(k, carry):
        given = resb[k]
        for half in range(2):
            rows = pl.ds(pl.multiple_of(half * 128 + k * 16, 16), 16)
            for side in range(2):
                lanes = slice(side * 128, side * 128 + 128)
                at = first[rows, lanes]
                forcing = jnp.where(at >= 0, take(given, jnp.maximum(at, 0)), 0.0)
                for m in range(2):
                    high, low = split(ens[m, rows, lanes].astype(f32) * forcing)
                    vhi[m, rows, lanes] = high
                    vlo[m, rows, lanes] = low
        return carry

    lax.fori_loop(0, 8, place, 0)
    copies = begin(1)
    update = finish(1, copies)
    for m in range(2):
        ctl[m] = ctl[m] + w0[m] + update[:, m * TILE : (m + 1) * TILE]
    store = pltpu.make_async_copy(ctl, out, load_sem.at[0])
    store.start()
    for copy in sends:
        copy.wait_send()
    store.wait()


def on_device(control, ensemble, obs_index, obs_value, obs_weight):
    vmem, dma = pltpu.VMEM, pltpu.SemaphoreType.DMA
    square = (TILE, TILE)
    return pl.pallas_call(
        kernel,
        out_shape=jax.ShapeDtypeStruct((2, TILE, TILE), f32),
        in_specs=[pl.BlockSpec(memory_space=pl.ANY)] * 5,
        out_specs=pl.BlockSpec(memory_space=pl.ANY),
        scratch_shapes=[
            vmem((2,) + square, f32), vmem((2,) + square, bf16), vmem((TILE, OBS), i32),
            vmem((2, 16, OBS), f32), vmem((2, 16, OBS), f32),
            vmem(square, bf16), vmem(square, bf16), vmem((2,) + square, bf16), vmem((2,) + square, bf16),
            vmem((2,) + square, f32), vmem(square, f32), vmem((128, 128), i32), vmem(square, i32),
            vmem((2, 8, 384), f32), vmem((2, 4, 8, 384), f32), vmem((2, 4, 8, 384), f32), vmem((2, 15, 8, 128), f32),
            vmem((8, 16, 128), f32), vmem((7, 16, 128), f32), vmem((16, 128), f32), vmem((3, 16, 128), f32), vmem((8, 16, 128), f32),
            dma((7,)), dma((2, 15)), dma((2, 15)), dma((7,)), dma((7,)), dma((3,)), dma((3,)), dma((7,)), dma((7,)),
        ],
        compiler_params=pltpu.CompilerParams(collective_id=0, has_side_effects=True),
    )(control, ensemble, obs_index, obs_value, obs_weight)


def solution(mesh):
    return jax.shard_map(
        on_device,
        mesh=mesh,
        in_specs=(
            P("mem", "gx", "gy"),
            P("mem", "gx", "gy"),
            P("gx", "gy"),
            P("gx", "gy"),
            P("gx", "gy"),
        ),
        out_specs=P("mem", "gx", "gy"),
        check_vma=False,
    )
```

time: 677 us -> 51.3 us (0.08)
  waiting for transfers between devices: 336 us -> 0 us
  other arithmetic: 114 us -> 0 us
  local copies, waits for them, and re-layouts: 112 us -> 5.08 us
  starting transfers between devices: 88.2 us -> 0 us
  Pallas kernels: 0 us -> 45.9 us
  between operations: 13.9 us -> 0.01 us
  matrix products: 12.1 us -> 0 us
    psum x1 -> x0, waiting for transfers between devices: 289 us -> none  [on_device(): increment = lax.psum(partial_value, 'mem')]
    unnamed x4 -> x0, other arithmetic: 114 us -> none
    gather x3 -> x0, local copies, waits for them, and re-layouts: 109 us -> none  [obs_residual(): picked = jnp.take_along_axis(grid_field, columns, axis=1)]
    ppermute x24 -> x0, starting transfers between devices: 88.2 us -> none  [from_behind(): lax.ppermute(value, axis, [(source, source + steps) for source in range(l...]
    ppermute x24 -> x0, waiting for transfers between devices: 46.8 us -> none  [from_behind(): lax.ppermute(value, axis, [(source, source + steps) for source in range(l...]
    pallas_call x0 -> x1, Pallas kernels: none -> 45.9 us  [on_device(): pl.pallas_call(kernel, out_shape=jax.ShapeDtypeStruct((2, TILE, TILE), f3...]
    dot_general x16 -> x0, matrix products: 12.1 us -> none  [the longest x2 2.08 us: sweep_x_backward(): jnp.einsum('ji,mjc->mic', forward_matrix, grid_field, precision=highest)]
  transfers between devices with their start and end apart: 25 -> 0, of which waited for: 23 -> 0; matrix products, arithmetic and copies ran while one was open for 1% -> 0% of each run, Pallas kernels for 0% -> 0%
where the time goes in v1:
time: 51.3 us; the launch traced here: 51 us
  Pallas kernels  45.9 us (89%)
  local copies, waits for them, and re-layouts  5.08 us (10%)
    pallas_call x1, Pallas kernels, on_device(): pl.pallas_call(kernel, out_shape=jax.ShapeDtypeStruct((2, TILE, TILE), f3...  45.9 us
    unnamed x8, local copies, waits for them, and re-layouts  5.08 us

profile of v1, /device:TPU:1, one launch (start us, length us, event | category | flops | bytes accessed | tf_op | source)
XLA Modules:
  0.0 51.0 jit_solution(9945669087496615543)
XLA Ops:
  0.0 0.0 copy-start
  0.0 1.6 %copy.6.obs_index = s32[256,64]{1,0:T(8,128)} copy(s32[256,64]{0,1:T(8,128)} %param.7) | data formatting | bytes 131072 | tf_op args[2]
  1.6 0.0 copy-done
  1.6 0.0 copy-start.1
  1.6 0.8 %copy.7.obs_value = f32[256,64]{1,0:T(8,128)} copy(f32[256,64]{0,1:T(8,128)S(1)} %copy-done) | data formatting | bytes 131072 | tf_op args[3]
  2.4 0.1 copy-done.1
  2.5 0.7 %copy.8.obs_weight = f32[256,64]{1,0:T(8,128)} copy(f32[256,64]{0,1:T(8,128)S(1)} %copy-done.1) | data formatting | bytes 131072 | tf_op args[4]
  3.2 45.9 %shard_map.55 = f32[2,256,256]{2,1,0:T(8,128)} custom-call(f32[2,256,256]{2,1,0:T(8,128)} %control.1, bf16[2,256,256]{2,1,0:T(8,128)(2,1)} %ensemble.1, s32[256,64]{1,0:T(8,128)} %copy.6.obs_index, f32[256,64]{1,0:T(8,128)} %copy.7.obs_value, f32[256,64]{1,0:T(8,128)} %copy.8.obs_weight), custom_call_target="tpu_custom_call" | custom-call | tf_op jit(solution)/shard_map/pallas_call | solution.py:335
  49.2 1.9 %copy.10 = f32[2,256,256]{2,1,0:T(8,128)} copy(f32[2,256,256]{2,1,0:T(8,128)} %shard_map.55) | data formatting | bytes 1048576
Async XLA Ops:
  0.0 1.6 %copy-start = (f32[256,64]{0,1:T(8,128)S(1)}, f32[256,64]{0,1:T(8,128)}, u32[]{:S(2)}) copy-start(f32[256,64]{0,1:T(8,128)} %param.8) | copy-start | bytes 196612
  1.6 0.8 %copy-start.1 = (f32[256,64]{0,1:T(8,128)S(1)}, f32[256,64]{0,1:T(8,128)}, u32[]{:S(2)}) copy-start(f32[256,64]{0,1:T(8,128)} %param.9) | copy-start | bytes 196612

commit v2 on v1

v2 whole, which is shorter than its diff:
```python
import functools
import math

import jax
import jax.numpy as jnp
from jax import lax
from jax.experimental import pallas as pl
from jax.experimental.pallas import tpu as pltpu
from jax.sharding import PartitionSpec as P

LEN = 400
TILE = 256
GRID = 4
RING = 16
NX = GRID * TILE
OBS = 64
saturation = 1.5
MESH = pl.DeviceIdType.MESH
f32 = jnp.float32
bf16 = jnp.bfloat16
i32 = jnp.int32
FAR = 1 << 20

CORNERS = [(dx, dy) for dy in (2, 1, 3) for dx in (2, 3, 1)]
LINES = [(0, 2), (0, 1), (0, 3), (2, 0), (3, 0), (1, 0)]
AROUND = [(dz, dx) for dz in (8, -7, 7, -6, 6, -5, 5, -4, 4, -3, 3, -2, 2, -1, 1, 0) for dx in (1, 0)][:-1]
BACK = [(dz, dx) for dz in (-4, -3, 3, -2, 2, -1, 1, 0) for dx in (1, 0)][:-1]
NEAR = [(dz, dx) for dz in (-2, 2, -1, 1, 0) for dx in (1, 0)][:-1]
PIECES = 16
ROWS = 8


def pair_scale():
    decay_rate = math.exp(-1.0 / LEN)
    return (1.0 - decay_rate * decay_rate) / (1.0 + decay_rate * decay_rate)


def decay(steps):
    return jnp.exp(steps.astype(f32) * (-1.0 / LEN))


def split(x):
    high = x.astype(bf16)
    return high, (x - high.astype(f32)).astype(bf16)


def dot(a, b, left=1, right=0):
    return lax.dot_general(a, b, (((left,), (right,)), ((), ())), preferred_element_type=f32)


def take(x, lanes):
    return jnp.take_along_axis(x, lanes, axis=1)


def iota(shape, dim):
    return lax.broadcasted_iota(i32, shape, dim)


def in_plane(dx, dy):
    return {
        "gx": lax.rem(lax.axis_index("gx") + dx, GRID),
        "gy": lax.rem(lax.axis_index("gy") + dy, GRID),
    }


def in_mem(dz, dx):
    mem = lax.axis_index("mem")
    z, half = lax.rem(mem, RING), mem // RING
    return {"mem": lax.rem(half + dx, 2) * RING + lax.rem(z + dz + RING, RING)}


def piece_of(dz, dx):
    mem = lax.axis_index("mem")
    z, half = lax.rem(mem, RING), mem // RING
    piece = lax.rem(z + dz + RING, PIECES // 2) * 2 + lax.rem(half + dx, 2)
    return pl.ds(pl.multiple_of(piece * ROWS, ROWS), ROWS)


def send(src, dst, send_sem, recv_sem, peer):
    pltpu.make_async_remote_copy(
        src, dst, send_sem, recv_sem, device_id=peer, device_id_type=MESH
    ).start()


def arrived(ref, sem):
    pltpu.make_async_copy(ref, ref, sem).wait()


def coefficients(axis, d, even, shape):
    me = lax.axis_index(axis)
    it = lax.rem(me - d + GRID, GRID)
    before = jnp.where(it < me, TILE * (me - it - 1) + 1, FAR)
    after = jnp.where(it > me, TILE * (it - me - 1) + 1, FAR)
    ends = 2 * NX - TILE * (me + it + 2) + 2
    own = decay(jnp.where(even, before, after))
    above = jnp.where(even, 0.0, -decay(jnp.full(shape, ends, i32)))
    return own, above


def kernel(
    control, ensemble, obs_index, obs_value, obs_weight, field, side_a, side_b,
    ctl, ens, idx, val, wgt, thi, tlo, vhi, vlo, w0, part, idxp, first,
    msg, lines, corners, pkb, gat, resb, valp, wgtp,
    load_sem, line_send, line_recv, corner_send, corner_recv, sum_send, sum_recv, back_send, back_recv,
    second, third,
):
    loads = [
        pltpu.make_async_copy(control, ctl, load_sem.at[0]),
        pltpu.make_async_copy(obs_index, idx, load_sem.at[1]),
        pltpu.make_async_copy(ensemble, ens, load_sem.at[2]),
        pltpu.make_async_copy(obs_value, val, load_sem.at[3]),
        pltpu.make_async_copy(obs_weight, wgt, load_sem.at[4]),
    ]
    for copy in loads:
        copy.start()
    barrier = pltpu.get_barrier_semaphore()
    peers = [in_plane(*o) for o in CORNERS + LINES] + [in_mem(*o) for o in NEAR]
    for peer in peers:
        pl.semaphore_signal(barrier, 1, device_id=peer, device_id_type=MESH)

    own = piece_of(0, 0)
    square = (TILE, TILE)
    table = decay(jnp.abs(iota(square, 0) - iota(square, 1)))
    high, low = split(table)
    thi[...] = high
    tlo[...] = low
    wide = (8, TILE)
    row, column = iota(wide, 0), iota(wide, 1)
    even = (row & 1) == 0
    ends = decay(jnp.where(even, TILE - 1 - column, column))
    starts = decay(jnp.where(even, column, TILE - 1 - column))
    f_row, b_row = ends[0:1], ends[1:2]
    ends_hi = ends.astype(bf16).astype(f32)
    ends16 = jnp.concatenate([ends_hi, ends - ends_hi], axis=0).astype(bf16)
    narrow = (8, 128)
    lane = iota(narrow, 1)
    left = lane < 64
    left16 = iota((16, 128), 1) < 64
    cx = [coefficients("gx", d, even, wide) for d in range(GRID)]
    cy = [coefficients("gy", d, even, wide) for d in range(GRID)]
    cl = [coefficients("gy", d, left, narrow) for d in range(GRID)]

    def fold(x):
        return x[0:8] + x[8:16]

    def summarize(turn):
        sums = []
        for side in range(2):
            for m in range(2):
                sums.append(fold(dot(ends16, vhi[m], 1, side) + dot(ends16, vlo[m], 1, side)))
        x = jnp.where(row < 2, sums[0], jnp.where(row < 4, sums[1], jnp.where(row < 6, sums[2], sums[3])))
        x_hi = x.astype(bf16).astype(f32)
        x16 = jnp.concatenate([x_hi, x - x_hi], axis=0).astype(bf16)
        corner_f = jnp.sum(x * f_row, axis=1, keepdims=True)
        corner_b = jnp.sum(x * b_row, axis=1, keepdims=True)
        msg[turn, :, 0:TILE] = fold(dot(x16, thi[...]) + dot(x16, tlo[...]))
        msg[turn, :, TILE:] = jnp.where(left, corner_f, corner_b)

    def share(turn):
        for n, o in enumerate(CORNERS):
            send(
                msg.at[turn, :, pl.ds(TILE, 128)], corners.at[turn, n],
                corner_send.at[turn], corner_recv.at[turn], in_plane(*o),
            )
        for n, o in enumerate(LINES):
            send(msg.at[turn], lines.at[turn, n], line_send.at[turn], line_recv.at[turn], in_plane(*o))

    def local(m):
        u = dot(thi[...], vhi[m]) + dot(tlo[...], vhi[m]) + dot(thi[...], vlo[m])
        uhi, ulo = split(u)
        return dot(uhi, thi[...]) + dot(ulo, thi[...]) + dot(uhi, tlo[...])

    def remote(turn):
        arrived(corners.at[turn], corner_recv.at[turn])
        arrived(lines.at[turn], line_recv.at[turn])

        def block(dx, dy):
            if (dx, dy) == (0, 0):
                return msg[turn]
            return lines[turn, LINES.index((dx, dy))]

        def weigh(c, x):
            return c[0] * x + c[1] * pltpu.roll(x, 1, 0)

        xs, ys, corner = 0.0, 0.0, 0.0
        for d in range(GRID):
            xs = xs + weigh(cx[d], block(d, 0)[:, 0:TILE])
            ys = ys + weigh(cy[d], block(0, d)[:, 0:TILE])
        for dy in range(GRID):
            over_x = 0.0
            for dx in range(GRID):
                if dx and dy:
                    g = corners[turn, CORNERS.index((dx, dy))]
                else:
                    g = block(dx, dy)[:, TILE:]
                over_x = over_x + weigh((cx[dx][0][:, 0:128], cx[dx][1][:, 0:128]), g)
            corner = corner + cl[dy][0] * over_x + cl[dy][1] * pltpu.roll(over_x, 64, 1)
        ab = jnp.where(row < 4, xs + corner[:, 0:1] * b_row + corner[:, 64:65] * f_row, ys)
        a = jnp.where(row < 4, starts, ab)
        b = jnp.where(row < 4, ab, starts)
        b = jnp.concatenate([jnp.where((row & 2) == 0, b, 0.0), jnp.where((row & 2) == 0, 0.0, b)], axis=1)
        a_hi, b_hi = a.astype(bf16).astype(f32), b.astype(bf16).astype(f32)
        a_lo, b_lo = a - a_hi, b - b_hi
        a = jnp.concatenate([a_hi, a_hi, a_lo, a_lo], axis=0).astype(bf16)
        b = jnp.concatenate([b_hi, b_lo, b_hi, b_lo], axis=0).astype(bf16)
        return a, b

    def pack(ref):
        return jnp.concatenate([ref[:, 0:128], ref[:, 128:256]], axis=0).T

    loads[0].wait()
    for m in range(2):
        high, low = split(ctl[m])
        vhi[m] = high
        vlo[m] = low
    summarize(0)
    pl.semaphore_wait(barrier, len(peers))
    for dz in (-2, 2):
        pl.semaphore_signal(second, 1, device_id=in_mem(dz, 0), device_id_type=MESH)
    share(0)
    for m in range(2):
        w0[m] = local(m)
    loads[1].wait()
    idxp[...] = pack(idx)
    loads[2].wait()
    pl.semaphore_wait(second, 2)
    for dz in (-4, 4):
        pl.semaphore_signal(third, 1, device_id=in_mem(dz, 0), device_id_type=MESH)
    a, b = remote(0)
    update = dot(a, b, 0, 0)
    part[...] = (
        ens[0].astype(f32) * (w0[0] + update[:, 0:TILE])
        + ens[1].astype(f32) * (w0[1] + update[:, TILE:])
    )

    def pick(k, carry):
        top = pl.ds(pl.multiple_of(k * 16, 16), 16)
        bottom = pl.ds(pl.multiple_of(128 + k * 16, 16), 16)
        at = idxp[top, :]
        low = at & 127
        upper = at >= 128
        above = jnp.where(upper, take(part[top, 128:256], low), take(part[top, 0:128], low))
        below = jnp.where(upper, take(part[bottom, 128:256], low), take(part[bottom, 0:128], low))
        pkb[top, :] = jnp.where(left16, above, below)
        return carry

    lax.fori_loop(0, 8, pick, 0, unroll=4)

    pl.semaphore_wait(third, 2)
    for n, o in enumerate(AROUND):
        send(pkb.at[piece_of(*o)], gat.at[n], sum_send, sum_recv, in_mem(*o))

    at = idxp[own, :]
    link = jnp.full(narrow, -1, i32)
    for j in range(OBS):
        here = jnp.where(left, at[:, j : j + 1], at[:, OBS + j : OBS + j + 1])
        there = jnp.where(left, j, OBS + j)
        link = jnp.where((here == at) & (lane > there), there, link)
    links = []
    for level in range(6):
        links.append(link)
        link = jnp.where(link >= 0, take(link, jnp.maximum(link, 0)), -1)
    loads[3].wait()
    loads[4].wait()
    valp[...] = pack(val)
    wgtp[...] = pack(wgt)
    value = valp[own, :]
    weight = wgtp[own, :] * (saturation * pair_scale())

    def find(k, carry):
        at = idxp[pl.ds(pl.multiple_of(k * 8, 8), 8), :]
        found = [jnp.full(narrow, -1, i32) for _ in range(4)]
        for j in range(OBS):
            for half in range(2):
                here = jnp.broadcast_to(at[:, half * OBS + j : half * OBS + j + 1], narrow)
                found[half * 2] = jnp.where(here == lane, half * OBS + j, found[half * 2])
                found[half * 2 + 1] = jnp.where(here == lane + 128, half * OBS + j, found[half * 2 + 1])
        for half in range(2):
            rows = pl.ds(pl.multiple_of(half * 128 + k * 8, 8), 8)
            first[rows, 0:128] = found[half * 2]
            first[rows, 128:256] = found[half * 2 + 1]
        return carry

    lax.fori_loop(0, 16, find, 0)

    arrived(gat, sum_recv)
    total = pkb[own, :] + jnp.sum(gat[...], axis=0)
    misfit = pair_scale() * total - value
    residual = weight * jnp.tanh(misfit * (1.0 / saturation))
    for link in links:
        residual = residual + jnp.where(link >= 0, take(residual, jnp.maximum(link, 0)), 0.0)
    resb[own, :] = residual
    for o in BACK:
        send(resb.at[own], resb.at[own], back_send, back_recv, in_mem(*o))
    others = resb.at[pl.ds(0, ROWS * len(BACK))]
    arrived(others, back_recv)

    def place(k, carry):
        given = resb[pl.ds(pl.multiple_of(k * 16, 16), 16), :]
        for half in range(2):
            rows = pl.ds(pl.multiple_of(half * 128 + k * 16, 16), 16)
            for side in range(2):
                lanes = slice(side * 128, side * 128 + 128)
                at = first[rows, lanes]
                forcing = jnp.where(at >= 0, take(given, jnp.maximum(at, 0)), 0.0)
                for m in range(2):
                    high, low = split(ens[m, rows, lanes].astype(f32) * forcing)
                    vhi[m, rows, lanes] = high
                    vlo[m, rows, lanes] = low
        return carry

    lax.fori_loop(0, 8, place, 0, unroll=4)
    summarize(1)
    share(1)
    for m in range(2):
        field[m] = ctl[m] + local(m)
    arrived(gat, sum_send)
    arrived(others, back_send)
    for turn in range(2):
        arrived(corners.at[turn], corner_send.at[turn])
        arrived(lines.at[turn], line_send.at[turn])
    a, b = remote(1)
    side_a[...] = a
    side_b[...] = b


def join(field, side_a, side_b, out, both, sem):
    copies = []
    for half in range(2):
        rows = slice(half * 128, half * 128 + 128)
        update = dot(side_a[:, rows], side_b[...], 0, 0)
        for m in range(2):
            both[m, rows, :] = field[m, rows, :] + update[:, m * TILE : (m + 1) * TILE]
            copy = pltpu.make_async_copy(both.at[m, rows, :], out.at[m, rows, :], sem.at[half, m])
            copy.start()
            copies.append(copy)
    for copy in copies:
        copy.wait()


def on_device(control, ensemble, obs_index, obs_value, obs_weight):
    vmem, dma = pltpu.VMEM, pltpu.SemaphoreType.DMA
    square = (TILE, TILE)
    packed = (128, 128)
    field, side_a, side_b = pl.pallas_call(
        kernel,
        out_shape=[vmem((2,) + square, f32), vmem((32, TILE), bf16), vmem((32, 2 * TILE), bf16)],
        in_specs=[pl.BlockSpec(memory_space=pltpu.HBM)] * 5,
        out_specs=[pl.BlockSpec(memory_space=vmem)] * 3,
        scratch_shapes=[
            vmem((2,) + square, f32), vmem((2,) + square, bf16),
            vmem((OBS, TILE), i32), vmem((OBS, TILE), f32), vmem((OBS, TILE), f32),
            vmem(square, bf16), vmem(square, bf16), vmem((2,) + square, bf16), vmem((2,) + square, bf16),
            vmem((2,) + square, f32), vmem(square, f32), vmem(packed, i32), vmem(square, i32),
            vmem((2, 8, 384), f32), vmem((2, len(LINES), 8, 384), f32), vmem((2, len(CORNERS), 8, 128), f32),
            vmem(packed, f32), vmem((len(AROUND), ROWS, 128), f32), vmem(packed, f32), vmem(packed, f32), vmem(packed, f32),
            dma((5,)), dma((2,)), dma((2,)), dma((2,)), dma((2,)), dma, dma, dma, dma,
            pltpu.SemaphoreType.REGULAR, pltpu.SemaphoreType.REGULAR,
        ],
        compiler_params=pltpu.CompilerParams(
            collective_id=0, has_side_effects=True, vmem_limit_bytes=24 << 20
        ),
    )(control, ensemble, obs_index.T, obs_value.T, obs_weight.T)
    return pl.pallas_call(
        join,
        out_shape=jax.ShapeDtypeStruct((2,) + square, f32),
        in_specs=[pl.BlockSpec(memory_space=vmem)] * 3,
        out_specs=pl.BlockSpec(memory_space=pl.ANY),
        scratch_shapes=[vmem((2,) + square, f32), dma((2, 2))],
        compiler_params=pltpu.CompilerParams(vmem_limit_bytes=8 << 20),
    )(field, side_a, side_b)


def solution(mesh):
    return jax.shard_map(
        on_device,
        mesh=mesh,
        in_specs=(
            P("mem", "gx", "gy"),
            P("mem", "gx", "gy"),
            P("gx", "gy"),
            P("gx", "gy"),
            P("gx", "gy"),
        ),
        out_specs=P("mem", "gx", "gy"),
        check_vma=False,
    )
```

time: 51.3 us -> 48.1 us (0.938)
  Pallas kernels: 45.9 us -> 43.3 us
  local copies, waits for them, and re-layouts: 5.08 us -> 4.51 us
    pallas_call x1 -> x2, Pallas kernels: 45.9 us -> 43.3 us  [the longest x1 42.2 us: on_device(): pl.pallas_call(kernel, out_shape=[vmem((2,) + square, f32), vmem((32, TIL...]
    unnamed x8 -> x10, local copies, waits for them, and re-layouts: 5.08 us -> 4.51 us
where the time goes in v2:
time: 48.1 us; the launch traced here: 47.8 us
  Pallas kernels  43.3 us (90%)
  local copies, waits for them, and re-layouts  4.51 us (9%)
    pallas_call x1, Pallas kernels, on_device(): pl.pallas_call(kernel, out_shape=[vmem((2,) + square, f32), vmem((32, TIL...  42.2 us
    unnamed x10, local copies, waits for them, and re-layouts  4.51 us
    pallas_call x1, Pallas kernels, on_device(): pl.pallas_call(join, out_shape=jax.ShapeDtypeStruct((2,) + square, f32),...  1.03 us

profile of v2, /device:TPU:1, one launch (start us, length us, event | category | flops | bytes accessed | tf_op | source)
XLA Modules:
  0.0 47.8 jit_solution(8733346361056384660)
XLA Ops:
  0.0 0.0 copy-start
  0.0 1.0 %copy-done = f32[2,256,256]{2,1,0:T(8,128)S(1)} copy-done((f32[2,256,256]{2,1,0:T(8,128)S(1)}, f32[2,256,256]{2,1,0:T(8,128)}, u32[]{:S(2)}) %copy-start) | copy-done | bytes 524312
  1.0 0.0 copy-start.1
  1.0 0.9 %copy-done.1 = bf16[2,256,256]{2,1,0:T(8,128)(2,1)S(1)} copy-done((bf16[2,256,256]{2,1,0:T(8,128)(2,1)S(1)}, bf16[2,256,256]{2,1,0:T(8,128)(2,1)}, u32[]{:S(2)}) %copy-start.1) | copy-done | bytes 262168
  2.0 0.0 copy-start.2
  2.0 0.8 %copy-done.2 = s32[256,64]{0,1:T(8,128)S(1)} copy-done((s32[256,64]{0,1:T(8,128)S(1)}, s32[256,64]{0,1:T(8,128)}, u32[]{:S(2)}) %copy-start.2) | copy-done | bytes 65560
  2.8 0.0 copy-start.3
  2.8 0.8 %copy-done.3 = f32[256,64]{0,1:T(8,128)S(1)} copy-done((f32[256,64]{0,1:T(8,128)S(1)}, f32[256,64]{0,1:T(8,128)}, u32[]{:S(2)}) %copy-start.3) | copy-done | bytes 65560
  3.7 0.0 copy-start.4
  3.7 0.8 %copy-done.4 = f32[256,64]{0,1:T(8,128)S(1)} copy-done((f32[256,64]{0,1:T(8,128)S(1)}, f32[256,64]{0,1:T(8,128)}, u32[]{:S(2)}) %copy-start.4) | copy-done | bytes 65560
  4.5 42.2 %shard_map.55 = (f32[2,256,256]{2,1,0:T(8,128)S(1)}, bf16[32,256]{1,0:T(8,128)(2,1)S(1)}, bf16[32,512]{1,0:T(8,128)(2,1)S(1)}) custom-call(f32[2,256,256]{2,1,0:T(8,128)S(1)} %copy-done, bf16[2,256,256]{2,1,0:T(8,128)(2,1)S(1)} %copy-done.1, s32[64,256]{1,0:T(8,128)S(1)} %bitcast.3, f32[64,256]{1,0:T(8,128)S(1)} %bitcast.4, f32[64,256]{1,0:T(8,128)S(1)} %bitcast.5), custom_call_target="tpu_custom_call" | custom-call | tf_op jit(solution)/shard_map/pallas_call | solution.py:345
  46.8 1.0 %shard_map.56 = f32[2,256,256]{2,1,0:T(8,128)} custom-call(f32[2,256,256]{2,1,0:T(8,128)S(1)} %get-tuple-element.8.field, bf16[32,256]{1,0:T(8,128)(2,1)S(1)} %get-tuple-element.9.side_a, bf16[32,512]{1,0:T(8,128)(2,1)S(1)} %get-tuple-element.10.side_b), custom_call_target="tpu_custom_call" | custom-call | tf_op jit(solution)/shard_map/pallas_call | solution.py:364
Async XLA Ops:
  0.0 1.0 %copy-start = (f32[2,256,256]{2,1,0:T(8,128)S(1)}, f32[2,256,256]{2,1,0:T(8,128)}, u32[]{:S(2)}) copy-start(f32[2,256,256]{2,1,0:T(8,128)} %control.1) | copy-start | bytes 1572868
  1.0 0.9 %copy-start.1 = (bf16[2,256,256]{2,1,0:T(8,128)(2,1)S(1)}, bf16[2,256,256]{2,1,0:T(8,128)(2,1)}, u32[]{:S(2)}) copy-start(bf16[2,256,256]{2,1,0:T(8,128)(2,1)} %ensemble.1) | copy-start | bytes 786436
  2.0 0.8 %copy-start.2 = (s32[256,64]{0,1:T(8,128)S(1)}, s32[256,64]{0,1:T(8,128)}, u32[]{:S(2)}) copy-start(s32[256,64]{0,1:T(8,128)} %param.7) | copy-start | bytes 196612
  2.8 0.8 %copy-start.3 = (f32[256,64]{0,1:T(8,128)S(1)}, f32[256,64]{0,1:T(8,128)}, u32[]{:S(2)}) copy-start(f32[256,64]{0,1:T(8,128)} %param.8) | copy-start | bytes 196612
  3.7 0.8 %copy-start.4 = (f32[256,64]{0,1:T(8,128)S(1)}, f32[256,64]{0,1:T(8,128)}, u32[]{:S(2)}) copy-start(f32[256,64]{0,1:T(8,128)} %param.9) | copy-start | bytes 196612

commit v3 on v2

--- a/solution.py
+++ b/solution.py
@@ -360,7 +360,10 @@
         compiler_params=pltpu.CompilerParams(
             collective_id=0, has_side_effects=True, vmem_limit_bytes=24 << 20
         ),
-    )(control, ensemble, obs_index.T, obs_value.T, obs_weight.T)
+    )(*(
+        pltpu.with_memory_space_constraint(x, pltpu.HBM)
+        for x in (control, ensemble, obs_index.T, obs_value.T, obs_weight.T)
+    ))
     return pl.pallas_call(
         join,
         out_shape=jax.ShapeDtypeStruct((2,) + square, f32),

time: 48.1 us -> 43.1 us (0.90)
  local copies, waits for them, and re-layouts: 4.51 us -> 0 us
    unnamed x10 -> x0, local copies, waits for them, and re-layouts: 4.51 us -> none
where the time goes in v3:
time: 43.1 us; the launch traced here: 43 us
  Pallas kernels  43 us (100%)
    pallas_call x1, Pallas kernels, on_device(): pl.pallas_call(kernel, out_shape=[vmem((2,) + square, f32), vmem((32, TIL...  41.9 us
    pallas_call x1, Pallas kernels, on_device(): pl.pallas_call(join, out_shape=jax.ShapeDtypeStruct((2,) + square, f32),...  1.03 us

profile of v3, /device:TPU:1, one launch (start us, length us, event | category | flops | bytes accessed | tf_op | source)
XLA Modules:
  0.0 43.0 jit_solution(2900350525252212287)
XLA Ops:
  0.0 41.9 %shard_map.55 = (f32[2,256,256]{2,1,0:T(8,128)S(1)}, bf16[32,256]{1,0:T(8,128)(2,1)S(1)}, bf16[32,512]{1,0:T(8,128)(2,1)S(1)}) custom-call(f32[2,256,256]{2,1,0:T(8,128)} %control.1, bf16[2,256,256]{2,1,0:T(8,128)(2,1)} %ensemble.1, s32[64,256]{1,0:T(8,128)} %bitcast.3, f32[64,256]{1,0:T(8,128)} %bitcast.4, f32[64,256]{1,0:T(8,128)} %bitcast.5), custom_call_target="tpu_custom_call" | custom-call | tf_op jit(solution)/shard_map/pallas_call | solution.py:345
  41.9 1.0 %shard_map.56 = f32[2,256,256]{2,1,0:T(8,128)} custom-call(f32[2,256,256]{2,1,0:T(8,128)S(1)} %get-tuple-element.8.field, bf16[32,256]{1,0:T(8,128)(2,1)S(1)} %get-tuple-element.9.side_a, bf16[32,512]{1,0:T(8,128)(2,1)S(1)} %get-tuple-element.10.side_b), custom_call_target="tpu_custom_call" | custom-call | tf_op jit(solution)/shard_map/pallas_call | solution.py:367

commit v4 on v3

--- a/solution.py
+++ b/solution.py
@@ -23,11 +23,12 @@
 
 CORNERS = [(dx, dy) for dy in (2, 1, 3) for dx in (2, 3, 1)]
 LINES = [(0, 2), (0, 1), (0, 3), (2, 0), (3, 0), (1, 0)]
-AROUND = [(dz, dx) for dz in (8, -7, 7, -6, 6, -5, 5, -4, 4, -3, 3, -2, 2, -1, 1, 0) for dx in (1, 0)][:-1]
-BACK = [(dz, dx) for dz in (-4, -3, 3, -2, 2, -1, 1, 0) for dx in (1, 0)][:-1]
-NEAR = [(dz, dx) for dz in (-2, 2, -1, 1, 0) for dx in (1, 0)][:-1]
-PIECES = 16
-ROWS = 8
+COLUMN = [8, -7, 7, -6, 6, -5, 5, -4, 4, -3, 3, -2, 2, -1, 1]
+BACK = [(dz, dx) for dz in (-4, -3, 3, -2, 2, -1, 1, 0) for dx in (1, 0)]
+NEAR = [(-4, 0), (4, 0), (-3, 0), (3, 0), (-2, 0), (2, 0), (0, 1), (-1, 0), (1, 0)]
+PIECES = 8
+ROWS = 16
+LEVELS = 6
 
 
 def pair_scale():
@@ -69,10 +70,8 @@
     return {"mem": lax.rem(half + dx, 2) * RING + lax.rem(z + dz + RING, RING)}
 
 
-def piece_of(dz, dx):
-    mem = lax.axis_index("mem")
-    z, half = lax.rem(mem, RING), mem // RING
-    piece = lax.rem(z + dz + RING, PIECES // 2) * 2 + lax.rem(half + dx, 2)
+def piece_of(dz):
+    piece = lax.rem(lax.axis_index("mem") + dz + RING, PIECES)
     return pl.ds(pl.multiple_of(piece * ROWS, ROWS), ROWS)
 
 
@@ -99,26 +98,35 @@
 
 def kernel(
     control, ensemble, obs_index, obs_value, obs_weight, field, side_a, side_b,
-    ctl, ens, idx, val, wgt, thi, tlo, vhi, vlo, w0, part, idxp, first,
-    msg, lines, corners, pkb, gat, resb, valp, wgtp,
+    ctl, ens, idx, val, wgt, thi, tlo, vhi, vlo, w0, part, idxp, first, nexts,
+    msg, lines, corners, pkb, gat, tot, res, valp, wgtp,
     load_sem, line_send, line_recv, corner_send, corner_recv, sum_send, sum_recv, back_send, back_recv,
-    second, third,
+    column_in, sibling_in, other_in, all_in,
 ):
     loads = [
-        pltpu.make_async_copy(control, ctl, load_sem.at[0]),
-        pltpu.make_async_copy(obs_index, idx, load_sem.at[1]),
-        pltpu.make_async_copy(ensemble, ens, load_sem.at[2]),
-        pltpu.make_async_copy(obs_value, val, load_sem.at[3]),
-        pltpu.make_async_copy(obs_weight, wgt, load_sem.at[4]),
+        pltpu.make_async_copy(control.at[0], ctl.at[0], load_sem.at[0]),
+        pltpu.make_async_copy(control.at[1], ctl.at[1], load_sem.at[1]),
+        pltpu.make_async_copy(obs_index, idx, load_sem.at[2]),
+        pltpu.make_async_copy(ensemble, ens, load_sem.at[3]),
+        pltpu.make_async_copy(obs_value, val, load_sem.at[4]),
+        pltpu.make_async_copy(obs_weight, wgt, load_sem.at[5]),
     ]
     for copy in loads:
         copy.start()
     barrier = pltpu.get_barrier_semaphore()
-    peers = [in_plane(*o) for o in CORNERS + LINES] + [in_mem(*o) for o in NEAR]
+    peers = [in_mem(*o) for o in NEAR] + [in_plane(*o) for o in CORNERS + LINES]
+
+    def signal(sem, peer):
+        pl.semaphore_signal(sem, 1, device_id=peer, device_id_type=MESH)
+
     for peer in peers:
-        pl.semaphore_signal(barrier, 1, device_id=peer, device_id_type=MESH)
-
-    own = piece_of(0, 0)
+        signal(barrier, peer)
+    gx = lax.axis_index("gx")
+    core = lax.rem(gx, 2)
+    half = lax.axis_index("mem") // RING
+    sibling = {"gx": gx + 1 - 2 * core}
+
+    own = piece_of(0)
     square = (TILE, TILE)
     table = decay(jnp.abs(iota(square, 0) - iota(square, 1)))
     high, low = split(table)
@@ -144,10 +152,16 @@
         return x[0:8] + x[8:16]
 
     def summarize(turn):
-        sums = []
-        for side in range(2):
-            for m in range(2):
+        over_x, over_y = [], []
+        for m in range(2):
+            if turn == 0:
+                loads[m].wait()
+                high, low = split(ctl[m])
+                vhi[m] = high
+                vlo[m] = low
+            for side, sums in enumerate((over_x, over_y)):
                 sums.append(fold(dot(ends16, vhi[m], 1, side) + dot(ends16, vlo[m], 1, side)))
+        sums = over_x + over_y
         x = jnp.where(row < 2, sums[0], jnp.where(row < 4, sums[1], jnp.where(row < 6, sums[2], sums[3])))
         x_hi = x.astype(bf16).astype(f32)
         x16 = jnp.concatenate([x_hi, x - x_hi], axis=0).astype(bf16)
@@ -208,24 +222,19 @@
     def pack(ref):
         return jnp.concatenate([ref[:, 0:128], ref[:, 128:256]], axis=0).T
 
-    loads[0].wait()
-    for m in range(2):
-        high, low = split(ctl[m])
-        vhi[m] = high
-        vlo[m] = low
     summarize(0)
     pl.semaphore_wait(barrier, len(peers))
-    for dz in (-2, 2):
-        pl.semaphore_signal(second, 1, device_id=in_mem(dz, 0), device_id_type=MESH)
+    for dz in (-4, 4):
+        signal(column_in, in_mem(dz, 0))
     share(0)
     for m in range(2):
         w0[m] = local(m)
-    loads[1].wait()
+    loads[2].wait()
     idxp[...] = pack(idx)
-    loads[2].wait()
-    pl.semaphore_wait(second, 2)
-    for dz in (-4, 4):
-        pl.semaphore_signal(third, 1, device_id=in_mem(dz, 0), device_id_type=MESH)
+    loads[3].wait()
+    pl.semaphore_wait(column_in, 2)
+    signal(sibling_in, sibling)
+    signal(other_in, in_mem(0, 1))
     a, b = remote(0)
     update = dot(a, b, 0, 0)
     part[...] = (
@@ -246,57 +255,83 @@
 
     lax.fori_loop(0, 8, pick, 0, unroll=4)
 
-    pl.semaphore_wait(third, 2)
-    for n, o in enumerate(AROUND):
-        send(pkb.at[piece_of(*o)], gat.at[n], sum_send, sum_recv, in_mem(*o))
-
-    at = idxp[own, :]
-    link = jnp.full(narrow, -1, i32)
-    for j in range(OBS):
-        here = jnp.where(left, at[:, j : j + 1], at[:, OBS + j : OBS + j + 1])
-        there = jnp.where(left, j, OBS + j)
-        link = jnp.where((here == at) & (lane > there), there, link)
-    links = []
-    for level in range(6):
-        links.append(link)
+    pl.semaphore_wait(sibling_in, 1)
+    for n, dz in enumerate(COLUMN):
+        send(
+            pkb.at[piece_of(dz)], gat.at[core, n], sum_send, sum_recv.at[core],
+            in_mem(dz, 0) | {"gx": gx + 1 - core},
+        )
+
+    @pl.when(core == 0)
+    def _():
+        send(pkb.at[own], gat.at[0, len(COLUMN)], sum_send, sum_recv.at[0], sibling)
+
+    @pl.when(core == 1)
+    def _():
+        gat[1, len(COLUMN)] = pkb[own, :]
+
+    def find(k, carry):
+        rows = pl.ds(pl.multiple_of((k // 2) * 128, 128), 128)
+        lanes = pl.ds(pl.multiple_of((k % 2) * 128, 128), 128)
+        cell = iota((128, 128), 0) + (k % 2) * 128
+        found = jnp.full((128, 128), -1, i32)
+        for j in range(OBS):
+            found = jnp.where(idx[j : j + 1, rows] == cell, (k // 2) * OBS + j, found)
+        first[rows, lanes] = found.T
+        return carry
+
+    lax.fori_loop(0, 4, find, 0)
+    level = iota(narrow, 0)
+    link = []
+    for side in range(2):
+        at = [idx[8 * t : 8 * t + 8, side * 128 : side * 128 + 128] for t in range(8)]
+        found = [jnp.full(narrow, -1, i32) for t in range(8)]
+        for j in range(OBS):
+            here = at[j // 8][j % 8 : j % 8 + 1]
+            for t in range(j // 8, 8):
+                hit = at[t] == here
+                if t == j // 8:
+                    hit = hit & (level > j % 8)
+                found[t] = jnp.where(hit, side * OBS + j, found[t])
+        link += found
+    link = jnp.concatenate(link, axis=0).T
+    for n in range(LEVELS):
+        nexts[n] = link
         link = jnp.where(link >= 0, take(link, jnp.maximum(link, 0)), -1)
-    loads[3].wait()
     loads[4].wait()
-    valp[...] = pack(val)
-    wgtp[...] = pack(wgt)
-    value = valp[own, :]
-    weight = wgtp[own, :] * (saturation * pair_scale())
-
-    def find(k, carry):
-        at = idxp[pl.ds(pl.multiple_of(k * 8, 8), 8), :]
-        found = [jnp.full(narrow, -1, i32) for _ in range(4)]
-        for j in range(OBS):
-            for half in range(2):
-                here = jnp.broadcast_to(at[:, half * OBS + j : half * OBS + j + 1], narrow)
-                found[half * 2] = jnp.where(here == lane, half * OBS + j, found[half * 2])
-                found[half * 2 + 1] = jnp.where(here == lane + 128, half * OBS + j, found[half * 2 + 1])
-        for half in range(2):
-            rows = pl.ds(pl.multiple_of(half * 128 + k * 8, 8), 8)
-            first[rows, 0:128] = found[half * 2]
-            first[rows, 128:256] = found[half * 2 + 1]
-        return carry
-
-    lax.fori_loop(0, 16, find, 0)
-
-    arrived(gat, sum_recv)
-    total = pkb[own, :] + jnp.sum(gat[...], axis=0)
-    misfit = pair_scale() * total - value
-    residual = weight * jnp.tanh(misfit * (1.0 / saturation))
-    for link in links:
+    loads[5].wait()
+    valp[...] = pack(val) * (1.0 / saturation)
+    wgtp[...] = pack(wgt) * (saturation * pair_scale())
+    pl.semaphore_wait(other_in, 1)
+    signal(all_in, sibling)
+    pl.semaphore_wait(all_in, 1)
+
+    @pl.when(core == 1)
+    def _():
+        for c in range(2):
+            arrived(gat.at[c, pl.ds(0, len(COLUMN) + 1 - c)], sum_recv.at[c])
+            tot[c] = jnp.sum(gat[c], axis=0)
+            for o in BACK:
+                if o != (0, 0):
+                    send(tot.at[c], res.at[half, own], back_send.at[c], back_recv, in_mem(*o) | {"gx": gx - 1 + c})
+                elif c == 0:
+                    send(tot.at[c], res.at[half, own], back_send.at[c], back_recv, sibling)
+        res[half, own, :] = tot[1]
+        arrived(gat.at[1, pl.ds(0, len(COLUMN))], back_recv)
+
+    @pl.when(core == 0)
+    def _():
+        arrived(res, back_recv)
+
+    total = res[0] + res[1]
+    residual = wgtp[...] * jnp.tanh(total * (pair_scale() / saturation) - valp[...])
+    for n in range(LEVELS):
+        link = nexts[n]
         residual = residual + jnp.where(link >= 0, take(residual, jnp.maximum(link, 0)), 0.0)
-    resb[own, :] = residual
-    for o in BACK:
-        send(resb.at[own], resb.at[own], back_send, back_recv, in_mem(*o))
-    others = resb.at[pl.ds(0, ROWS * len(BACK))]
-    arrived(others, back_recv)
+    part[0:128, 0:128] = residual
 
     def place(k, carry):
-        given = resb[pl.ds(pl.multiple_of(k * 16, 16), 16), :]
+        given = part[pl.ds(pl.multiple_of(k * 16, 16), 16), 0:128]
         for half in range(2):
             rows = pl.ds(pl.multiple_of(half * 128 + k * 16, 16), 16)
             for side in range(2):
@@ -314,8 +349,17 @@
     share(1)
     for m in range(2):
         field[m] = ctl[m] + local(m)
-    arrived(gat, sum_send)
-    arrived(others, back_send)
+
+    @pl.when(core == 0)
+    def _():
+        arrived(gat.at[0], sum_send)
+
+    @pl.when(core == 1)
+    def _():
+        arrived(gat.at[1, pl.ds(0, len(COLUMN))], sum_send)
+        for c in range(2):
+            arrived(gat.at[c, pl.ds(0, len(COLUMN) + 1 - c)], back_send.at[c])
+
     for turn in range(2):
         arrived(corners.at[turn], corner_send.at[turn])
         arrived(lines.at[turn], line_send.at[turn])
@@ -326,12 +370,12 @@
 
 def join(field, side_a, side_b, out, both, sem):
     copies = []
-    for half in range(2):
-        rows = slice(half * 128, half * 128 + 128)
+    for quarter in range(4):
+        rows = slice(quarter * 64, quarter * 64 + 64)
         update = dot(side_a[:, rows], side_b[...], 0, 0)
         for m in range(2):
             both[m, rows, :] = field[m, rows, :] + update[:, m * TILE : (m + 1) * TILE]
-            copy = pltpu.make_async_copy(both.at[m, rows, :], out.at[m, rows, :], sem.at[half, m])
+            copy = pltpu.make_async_copy(both.at[m, rows, :], out.at[m, rows, :], sem.at[quarter, m])
             copy.start()
             copies.append(copy)
     for copy in copies:
@@ -352,9 +396,12 @@
             vmem((OBS, TILE), i32), vmem((OBS, TILE), f32), vmem((OBS, TILE), f32),
             vmem(square, bf16), vmem(square, bf16), vmem((2,) + square, bf16), vmem((2,) + square, bf16),
             vmem((2,) + square, f32), vmem(square, f32), vmem(packed, i32), vmem(square, i32),
+            vmem((LEVELS,) + packed, i32),
             vmem((2, 8, 384), f32), vmem((2, len(LINES), 8, 384), f32), vmem((2, len(CORNERS), 8, 128), f32),
-            vmem(packed, f32), vmem((len(AROUND), ROWS, 128), f32), vmem(packed, f32), vmem(packed, f32), vmem(packed, f32),
-            dma((5,)), dma((2,)), dma((2,)), dma((2,)), dma((2,)), dma, dma, dma, dma,
+            vmem(packed, f32), vmem((2, RING, ROWS, 128), f32), vmem((2, ROWS, 128), f32), vmem((2,) + packed, f32),
+            vmem(packed, f32), vmem(packed, f32),
+            dma((6,)), dma((2,)), dma((2,)), dma((2,)), dma((2,)), dma, dma((2,)), dma((2,)), dma,
+            pltpu.SemaphoreType.REGULAR, pltpu.SemaphoreType.REGULAR,
             pltpu.SemaphoreType.REGULAR, pltpu.SemaphoreType.REGULAR,
         ],
         compiler_params=pltpu.CompilerParams(
@@ -369,7 +416,7 @@
         out_shape=jax.ShapeDtypeStruct((2,) + square, f32),
         in_specs=[pl.BlockSpec(memory_space=vmem)] * 3,
         out_specs=pl.BlockSpec(memory_space=pl.ANY),
-        scratch_shapes=[vmem((2,) + square, f32), dma((2, 2))],
+        scratch_shapes=[vmem((2,) + square, f32), dma((4, 2))],
         compiler_params=pltpu.CompilerParams(vmem_limit_bytes=8 << 20),
     )(field, side_a, side_b)
 

time: 43.1 us -> 41.4 us (0.961)
  Pallas kernels: 43 us -> 41.3 us
    pallas_call x1, Pallas kernels: 41.9 us -> 40.2 us  [on_device(): pl.pallas_call(kernel, out_shape=[vmem((2,) + square, f32), vmem((32, TIL...]
where the time goes in v4:
time: 41.4 us; the launch traced here: 41.3 us
  Pallas kernels  41.3 us (100%)
    pallas_call x1, Pallas kernels, on_device(): pl.pallas_call(kernel, out_shape=[vmem((2,) + square, f32), vmem((32, TIL...  40.2 us
    pallas_call x1, Pallas kernels, on_device(): pl.pallas_call(join, out_shape=jax.ShapeDtypeStruct((2,) + square, f32),...  1.08 us

profile of v4, /device:TPU:1, one launch (start us, length us, event | category | flops | bytes accessed | tf_op | source)
XLA Modules:
  0.0 41.3 jit_solution(13726390460336462244)
XLA Ops:
  0.0 40.2 %shard_map.55 = (f32[2,256,256]{2,1,0:T(8,128)S(1)}, bf16[32,256]{1,0:T(8,128)(2,1)S(1)}, bf16[32,512]{1,0:T(8,128)(2,1)S(1)}) custom-call(f32[2,256,256]{2,1,0:T(8,128)} %control.1, bf16[2,256,256]{2,1,0:T(8,128)(2,1)} %ensemble.1, s32[64,256]{1,0:T(8,128)} %bitcast.3, f32[64,256]{1,0:T(8,128)} %bitcast.4, f32[64,256]{1,0:T(8,128)} %bitcast.5), custom_call_target="tpu_custom_call" | custom-call | tf_op jit(solution)/shard_map/pallas_call | solution.py:389
  40.2 1.1 %shard_map.56 = f32[2,256,256]{2,1,0:T(8,128)} custom-call(f32[2,256,256]{2,1,0:T(8,128)S(1)} %get-tuple-element.8.field, bf16[32,256]{1,0:T(8,128)(2,1)S(1)} %get-tuple-element.9.side_a, bf16[32,512]{1,0:T(8,128)(2,1)S(1)} %get-tuple-element.10.side_b), custom_call_target="tpu_custom_call" | custom-call | tf_op jit(solution)/shard_map/pallas_call | solution.py:414

commit v5 on v4

--- a/solution.py
+++ b/solution.py
@@ -24,11 +24,12 @@
 CORNERS = [(dx, dy) for dy in (2, 1, 3) for dx in (2, 3, 1)]
 LINES = [(0, 2), (0, 1), (0, 3), (2, 0), (3, 0), (1, 0)]
 COLUMN = [8, -7, 7, -6, 6, -5, 5, -4, 4, -3, 3, -2, 2, -1, 1]
-BACK = [(dz, dx) for dz in (-4, -3, 3, -2, 2, -1, 1, 0) for dx in (1, 0)]
-NEAR = [(-4, 0), (4, 0), (-3, 0), (3, 0), (-2, 0), (2, 0), (0, 1), (-1, 0), (1, 0)]
+BACK = [(dz, dx) for dz in (-4, -3, 3, -2, 2, -1, 1, 0) for dx in (1, 0)][:-1]
+NEAR = [(-3, 0), (3, 0), (-2, 0), (2, 0), (0, 1), (-1, 0), (1, 0)]
 PIECES = 8
 ROWS = 16
 LEVELS = 6
+HALVES = [slice(0, 128), slice(128, 256)]
 
 
 def pair_scale():
@@ -50,7 +51,7 @@
 
 
 def take(x, lanes):
-    return jnp.take_along_axis(x, lanes, axis=1)
+    return jnp.take_along_axis(x, lanes, axis=1, mode="promise_in_bounds")
 
 
 def iota(shape, dim):
@@ -98,18 +99,21 @@
 
 def kernel(
     control, ensemble, obs_index, obs_value, obs_weight, field, side_a, side_b,
-    ctl, ens, idx, val, wgt, thi, tlo, vhi, vlo, w0, part, idxp, first, nexts,
-    msg, lines, corners, pkb, gat, tot, res, valp, wgtp,
+    ctl, ens, idx, val, wgt, thi, tlo, vhi, vlo, w0, idxp, first, nexts, fcol, bcol,
+    msg, lines, corners, pkb, gat, tot, res, valp, wgtp, at_ref,
     load_sem, line_send, line_recv, corner_send, corner_recv, sum_send, sum_recv, back_send, back_recv,
-    column_in, sibling_in, other_in, all_in,
+    near_in, column_in, other_in,
 ):
     loads = [
-        pltpu.make_async_copy(control.at[0], ctl.at[0], load_sem.at[0]),
-        pltpu.make_async_copy(control.at[1], ctl.at[1], load_sem.at[1]),
-        pltpu.make_async_copy(obs_index, idx, load_sem.at[2]),
-        pltpu.make_async_copy(ensemble, ens, load_sem.at[3]),
-        pltpu.make_async_copy(obs_value, val, load_sem.at[4]),
-        pltpu.make_async_copy(obs_weight, wgt, load_sem.at[5]),
+        pltpu.make_async_copy(control.at[m, rows, :], ctl.at[m, rows, :], load_sem.at[2 * m + n])
+        for m in range(2)
+        for n, rows in enumerate(HALVES)
+    ]
+    loads += [
+        pltpu.make_async_copy(obs_index, idx, load_sem.at[4]),
+        pltpu.make_async_copy(ensemble, ens, load_sem.at[5]),
+        pltpu.make_async_copy(obs_value, val, load_sem.at[6]),
+        pltpu.make_async_copy(obs_weight, wgt, load_sem.at[7]),
     ]
     for copy in loads:
         copy.start()
@@ -121,10 +125,8 @@
 
     for peer in peers:
         signal(barrier, peer)
-    gx = lax.axis_index("gx")
-    core = lax.rem(gx, 2)
+    mirror = 1 - 2 * lax.rem(lax.axis_index("gx"), 2)
     half = lax.axis_index("mem") // RING
-    sibling = {"gx": gx + 1 - 2 * core}
 
     own = piece_of(0)
     square = (TILE, TILE)
@@ -143,26 +145,28 @@
     narrow = (8, 128)
     lane = iota(narrow, 1)
     left = lane < 64
-    left16 = iota((16, 128), 1) < 64
     cx = [coefficients("gx", d, even, wide) for d in range(GRID)]
     cy = [coefficients("gy", d, even, wide) for d in range(GRID)]
     cl = [coefficients("gy", d, left, narrow) for d in range(GRID)]
 
+    down = iota((TILE, 128), 0)
+    fcol[...] = decay(TILE - 1 - down)
+    bcol[...] = decay(down)
+
     def fold(x):
         return x[0:8] + x[8:16]
 
-    def summarize(turn):
-        over_x, over_y = [], []
+    def line_sums(v, rows):
+        return [jnp.sum((v * col[rows, :]).reshape(-1, 8, 128), axis=0) for col in (fcol, bcol)]
+
+    def summarize(turn, over_x):
+        x = 0.0
         for m in range(2):
-            if turn == 0:
-                loads[m].wait()
-                high, low = split(ctl[m])
-                vhi[m] = high
-                vlo[m] = low
-            for side, sums in enumerate((over_x, over_y)):
-                sums.append(fold(dot(ends16, vhi[m], 1, side) + dot(ends16, vlo[m], 1, side)))
-        sums = over_x + over_y
-        x = jnp.where(row < 2, sums[0], jnp.where(row < 4, sums[1], jnp.where(row < 6, sums[2], sums[3])))
+            y = fold(dot(ends16, vhi[m], 1, 1) + dot(ends16, vlo[m], 1, 1))
+            x = jnp.where((row >> 1) == 2 + m, y, x)
+            for end in range(2):
+                line = jnp.concatenate([over_x[m][side][end] for side in range(2)], axis=1)
+                x = jnp.where(row == 2 * m + end, jnp.sum(line, axis=0, keepdims=True), x)
         x_hi = x.astype(bf16).astype(f32)
         x16 = jnp.concatenate([x_hi, x - x_hi], axis=0).astype(bf16)
         corner_f = jnp.sum(x * f_row, axis=1, keepdims=True)
@@ -222,53 +226,55 @@
     def pack(ref):
         return jnp.concatenate([ref[:, 0:128], ref[:, 128:256]], axis=0).T
 
-    summarize(0)
+    over_x = [[[0.0, 0.0] for side in range(2)] for m in range(2)]
+
+    def add_sums(m, side, v, rows):
+        over_x[m][side] = [old + new for old, new in zip(over_x[m][side], line_sums(v, rows))]
+
+    for m in range(2):
+        for n, rows in enumerate(HALVES):
+            loads[2 * m + n].wait()
+            high, low = split(ctl[m, rows, :])
+            vhi[m, rows, :] = high
+            vlo[m, rows, :] = low
+            for side, lanes in enumerate(HALVES):
+                add_sums(m, side, ctl[m, rows, lanes], rows)
+    summarize(0, over_x)
     pl.semaphore_wait(barrier, len(peers))
-    for dz in (-4, 4):
-        signal(column_in, in_mem(dz, 0))
+    for dz in (-3, 3):
+        signal(near_in, in_mem(dz, 0))
     share(0)
     for m in range(2):
         w0[m] = local(m)
-    loads[2].wait()
+    loads[4].wait()
     idxp[...] = pack(idx)
-    loads[3].wait()
+    loads[5].wait()
+    pl.semaphore_wait(near_in, 2)
+    for dz in (-2, 2):
+        signal(column_in, in_mem(dz, 0))
+    a, b = remote(0)
+    at_ref[...] = a.T
+    for k in range(4):
+        fields = []
+        for above in range(2):
+            rows = slice(above * 128 + k * 32, above * 128 + k * 32 + 32)
+            update = dot(at_ref[rows, :], b)
+            fields.append(
+                ens[0, rows, :].astype(f32) * (w0[0, rows, :] + update[:, 0:TILE])
+                + ens[1, rows, :].astype(f32) * (w0[1, rows, :] + update[:, TILE:])
+            )
+        for n in range(0, 32, 8):
+            rows = slice(n, n + 8)
+            at = idxp[k * 32 + n : k * 32 + n + 8, :]
+            low = at & 127
+            upper = at >= 128
+            picked = [jnp.where(upper, take(v[rows, 128:256], low), take(v[rows, 0:128], low)) for v in fields]
+            pkb[k * 32 + n : k * 32 + n + 8, :] = jnp.where(left, *picked)
+
     pl.semaphore_wait(column_in, 2)
-    signal(sibling_in, sibling)
     signal(other_in, in_mem(0, 1))
-    a, b = remote(0)
-    update = dot(a, b, 0, 0)
-    part[...] = (
-        ens[0].astype(f32) * (w0[0] + update[:, 0:TILE])
-        + ens[1].astype(f32) * (w0[1] + update[:, TILE:])
-    )
-
-    def pick(k, carry):
-        top = pl.ds(pl.multiple_of(k * 16, 16), 16)
-        bottom = pl.ds(pl.multiple_of(128 + k * 16, 16), 16)
-        at = idxp[top, :]
-        low = at & 127
-        upper = at >= 128
-        above = jnp.where(upper, take(part[top, 128:256], low), take(part[top, 0:128], low))
-        below = jnp.where(upper, take(part[bottom, 128:256], low), take(part[bottom, 0:128], low))
-        pkb[top, :] = jnp.where(left16, above, below)
-        return carry
-
-    lax.fori_loop(0, 8, pick, 0, unroll=4)
-
-    pl.semaphore_wait(sibling_in, 1)
     for n, dz in enumerate(COLUMN):
-        send(
-            pkb.at[piece_of(dz)], gat.at[core, n], sum_send, sum_recv.at[core],
-            in_mem(dz, 0) | {"gx": gx + 1 - core},
-        )
-
-    @pl.when(core == 0)
-    def _():
-        send(pkb.at[own], gat.at[0, len(COLUMN)], sum_send, sum_recv.at[0], sibling)
-
-    @pl.when(core == 1)
-    def _():
-        gat[1, len(COLUMN)] = pkb[own, :]
+        send(pkb.at[piece_of(dz)], gat.at[n], sum_send, sum_recv, in_mem(dz, 0))
 
     def find(k, carry):
         rows = pl.ds(pl.multiple_of((k // 2) * 128, 128), 128)
@@ -298,68 +304,43 @@
     for n in range(LEVELS):
         nexts[n] = link
         link = jnp.where(link >= 0, take(link, jnp.maximum(link, 0)), -1)
-    loads[4].wait()
-    loads[5].wait()
+    loads[6].wait()
+    loads[7].wait()
     valp[...] = pack(val) * (1.0 / saturation)
     wgtp[...] = pack(wgt) * (saturation * pair_scale())
     pl.semaphore_wait(other_in, 1)
-    signal(all_in, sibling)
-    pl.semaphore_wait(all_in, 1)
-
-    @pl.when(core == 1)
-    def _():
-        for c in range(2):
-            arrived(gat.at[c, pl.ds(0, len(COLUMN) + 1 - c)], sum_recv.at[c])
-            tot[c] = jnp.sum(gat[c], axis=0)
-            for o in BACK:
-                if o != (0, 0):
-                    send(tot.at[c], res.at[half, own], back_send.at[c], back_recv, in_mem(*o) | {"gx": gx - 1 + c})
-                elif c == 0:
-                    send(tot.at[c], res.at[half, own], back_send.at[c], back_recv, sibling)
-        res[half, own, :] = tot[1]
-        arrived(gat.at[1, pl.ds(0, len(COLUMN))], back_recv)
-
-    @pl.when(core == 0)
-    def _():
-        arrived(res, back_recv)
+    arrived(gat, sum_recv)
+    tot[...] = pkb[own, :] + jnp.sum(gat[...], axis=0)
+    for dz, dx in BACK:
+        send(tot, res.at[half, own], back_send, back_recv, in_mem(dz * mirror, dx))
+    res[half, own, :] = tot[...]
+    arrived(gat, back_recv)
 
     total = res[0] + res[1]
     residual = wgtp[...] * jnp.tanh(total * (pair_scale() / saturation) - valp[...])
     for n in range(LEVELS):
         link = nexts[n]
         residual = residual + jnp.where(link >= 0, take(residual, jnp.maximum(link, 0)), 0.0)
-    part[0:128, 0:128] = residual
-
-    def place(k, carry):
-        given = part[pl.ds(pl.multiple_of(k * 16, 16), 16), 0:128]
-        for half in range(2):
-            rows = pl.ds(pl.multiple_of(half * 128 + k * 16, 16), 16)
-            for side in range(2):
-                lanes = slice(side * 128, side * 128 + 128)
+    over_x = [[[0.0, 0.0] for side in range(2)] for m in range(2)]
+    for k in range(8):
+        given = residual[k * 16 : k * 16 + 16]
+        for above in range(2):
+            rows = slice(above * 128 + k * 16, above * 128 + k * 16 + 16)
+            for side, lanes in enumerate(HALVES):
                 at = first[rows, lanes]
                 forcing = jnp.where(at >= 0, take(given, jnp.maximum(at, 0)), 0.0)
                 for m in range(2):
-                    high, low = split(ens[m, rows, lanes].astype(f32) * forcing)
+                    v = ens[m, rows, lanes].astype(f32) * forcing
+                    high, low = split(v)
                     vhi[m, rows, lanes] = high
                     vlo[m, rows, lanes] = low
-        return carry
-
-    lax.fori_loop(0, 8, place, 0, unroll=4)
-    summarize(1)
+                    over_x[m][side] = [old + new for old, new in zip(over_x[m][side], line_sums(v, rows))]
+    summarize(1, over_x)
     share(1)
     for m in range(2):
         field[m] = ctl[m] + local(m)
-
-    @pl.when(core == 0)
-    def _():
-        arrived(gat.at[0], sum_send)
-
-    @pl.when(core == 1)
-    def _():
-        arrived(gat.at[1, pl.ds(0, len(COLUMN))], sum_send)
-        for c in range(2):
-            arrived(gat.at[c, pl.ds(0, len(COLUMN) + 1 - c)], back_send.at[c])
-
+    arrived(gat, sum_send)
+    arrived(gat, back_send)
     for turn in range(2):
         arrived(corners.at[turn], corner_send.at[turn])
         arrived(lines.at[turn], line_send.at[turn])
@@ -395,14 +376,13 @@
             vmem((2,) + square, f32), vmem((2,) + square, bf16),
             vmem((OBS, TILE), i32), vmem((OBS, TILE), f32), vmem((OBS, TILE), f32),
             vmem(square, bf16), vmem(square, bf16), vmem((2,) + square, bf16), vmem((2,) + square, bf16),
-            vmem((2,) + square, f32), vmem(square, f32), vmem(packed, i32), vmem(square, i32),
-            vmem((LEVELS,) + packed, i32),
+            vmem((2,) + square, f32), vmem(packed, i32), vmem(square, i32),
+            vmem((LEVELS,) + packed, i32), vmem((TILE, 128), f32), vmem((TILE, 128), f32),
             vmem((2, 8, 384), f32), vmem((2, len(LINES), 8, 384), f32), vmem((2, len(CORNERS), 8, 128), f32),
-            vmem(packed, f32), vmem((2, RING, ROWS, 128), f32), vmem((2, ROWS, 128), f32), vmem((2,) + packed, f32),
-            vmem(packed, f32), vmem(packed, f32),
-            dma((6,)), dma((2,)), dma((2,)), dma((2,)), dma((2,)), dma, dma((2,)), dma((2,)), dma,
-            pltpu.SemaphoreType.REGULAR, pltpu.SemaphoreType.REGULAR,
-            pltpu.SemaphoreType.REGULAR, pltpu.SemaphoreType.REGULAR,
+            vmem(packed, f32), vmem((len(COLUMN), ROWS, 128), f32), vmem((ROWS, 128), f32), vmem((2,) + packed, f32),
+            vmem(packed, f32), vmem(packed, f32), vmem((TILE, 32), bf16),
+            dma((8,)), dma((2,)), dma((2,)), dma((2,)), dma((2,)), dma, dma, dma, dma,
+            pltpu.SemaphoreType.REGULAR, pltpu.SemaphoreType.REGULAR, pltpu.SemaphoreType.REGULAR,
         ],
         compiler_params=pltpu.CompilerParams(
             collective_id=0, has_side_effects=True, vmem_limit_bytes=24 << 20

time: 41.4 us -> 40.7 us (0.983)
  Pallas kernels: 41.3 us -> 40.5 us
    pallas_call x1, Pallas kernels: 40.2 us -> 39.4 us  [on_device(): pl.pallas_call(kernel, out_shape=[vmem((2,) + square, f32), vmem((32, TIL...]
where the time goes in v5:
time: 40.7 us; the launch traced here: 40.5 us
  Pallas kernels  40.5 us (100%)
    pallas_call x1, Pallas kernels, on_device(): pl.pallas_call(kernel, out_shape=[vmem((2,) + square, f32), vmem((32, TIL...  39.4 us
    pallas_call x1, Pallas kernels, on_device(): pl.pallas_call(join, out_shape=jax.ShapeDtypeStruct((2,) + square, f32),...  1.08 us

profile of v5, /device:TPU:1, one launch (start us, length us, event | category | flops | bytes accessed | tf_op | source)
XLA Modules:
  0.0 40.5 jit_solution(11577631043681587155)
XLA Ops:
  0.0 39.4 %shard_map.55 = (f32[2,256,256]{2,1,0:T(8,128)S(1)}, bf16[32,256]{1,0:T(8,128)(2,1)S(1)}, bf16[32,512]{1,0:T(8,128)(2,1)S(1)}) custom-call(f32[2,256,256]{2,1,0:T(8,128)} %control.1, bf16[2,256,256]{2,1,0:T(8,128)(2,1)} %ensemble.1, s32[64,256]{1,0:T(8,128)} %bitcast.3, f32[64,256]{1,0:T(8,128)} %bitcast.4, f32[64,256]{1,0:T(8,128)} %bitcast.5), custom_call_target="tpu_custom_call" | custom-call | tf_op jit(solution)/shard_map/pallas_call | solution.py:370
  39.4 1.1 %shard_map.56 = f32[2,256,256]{2,1,0:T(8,128)} custom-call(f32[2,256,256]{2,1,0:T(8,128)S(1)} %get-tuple-element.8.field, bf16[32,256]{1,0:T(8,128)(2,1)S(1)} %get-tuple-element.9.side_a, bf16[32,512]{1,0:T(8,128)(2,1)S(1)} %get-tuple-element.10.side_b), custom_call_target="tpu_custom_call" | custom-call | tf_op jit(solution)/shard_map/pallas_call | solution.py:394

commit v6 on v5

--- a/solution.py
+++ b/solution.py
@@ -24,10 +24,12 @@
 CORNERS = [(dx, dy) for dy in (2, 1, 3) for dx in (2, 3, 1)]
 LINES = [(0, 2), (0, 1), (0, 3), (2, 0), (3, 0), (1, 0)]
 COLUMN = [8, -7, 7, -6, 6, -5, 5, -4, 4, -3, 3, -2, 2, -1, 1]
-BACK = [(dz, dx) for dz in (-4, -3, 3, -2, 2, -1, 1, 0) for dx in (1, 0)][:-1]
+AROUND = [(dz, dx) for dz in COLUMN + [0] for dx in (1, 0)][:-1]
+WINDOW = [(dz, dx) for dz in (-4, -3, 3, -2, 2, -1, 1, 0) for dx in (1, 0)][:-1]
 NEAR = [(-3, 0), (3, 0), (-2, 0), (2, 0), (0, 1), (-1, 0), (1, 0)]
 PIECES = 8
-ROWS = 16
+WIDE = 16
+THIN = 8
 LEVELS = 6
 HALVES = [slice(0, 128), slice(128, 256)]
 
@@ -71,9 +73,15 @@
     return {"mem": lax.rem(half + dx, 2) * RING + lax.rem(z + dz + RING, RING)}
 
 
-def piece_of(dz):
+def wide_piece(dz):
     piece = lax.rem(lax.axis_index("mem") + dz + RING, PIECES)
-    return pl.ds(pl.multiple_of(piece * ROWS, ROWS), ROWS)
+    return pl.ds(pl.multiple_of(piece * WIDE, WIDE), WIDE)
+
+
+def thin_piece(dz, dx):
+    mem = lax.axis_index("mem")
+    piece = lax.rem(mem + dz + RING, PIECES) * 2 + lax.rem(mem // RING + dx, 2)
+    return pl.ds(pl.multiple_of(piece * THIN, THIN), THIN)
 
 
 def send(src, dst, send_sem, recv_sem, peer):
@@ -100,9 +108,9 @@
 def kernel(
     control, ensemble, obs_index, obs_value, obs_weight, field, side_a, side_b,
     ctl, ens, idx, val, wgt, thi, tlo, vhi, vlo, w0, idxp, first, nexts, fcol, bcol,
-    msg, lines, corners, pkb, gat, tot, res, valp, wgtp, at_ref,
+    msg, lines, corners, pkb, gat, thin, tot, res, valp, wgtp, at_ref,
     load_sem, line_send, line_recv, corner_send, corner_recv, sum_send, sum_recv, back_send, back_recv,
-    near_in, column_in, other_in,
+    near_in, column_in, other_in, all_in,
 ):
     loads = [
         pltpu.make_async_copy(control.at[m, rows, :], ctl.at[m, rows, :], load_sem.at[2 * m + n])
@@ -118,17 +126,18 @@
     for copy in loads:
         copy.start()
     barrier = pltpu.get_barrier_semaphore()
-    peers = [in_mem(*o) for o in NEAR] + [in_plane(*o) for o in CORNERS + LINES]
+    peers = [in_plane(*o) for o in CORNERS] + [in_mem(*o) for o in NEAR] + [in_plane(*o) for o in LINES]
 
     def signal(sem, peer):
         pl.semaphore_signal(sem, 1, device_id=peer, device_id_type=MESH)
 
     for peer in peers:
         signal(barrier, peer)
-    mirror = 1 - 2 * lax.rem(lax.axis_index("gx"), 2)
-    half = lax.axis_index("mem") // RING
-
-    own = piece_of(0)
+    core = lax.rem(lax.axis_index("gx"), 2)
+    mem = lax.axis_index("mem")
+    half, turned = mem // RING, lax.rem(mem, RING) // PIECES
+
+    wide_own, thin_own = wide_piece(0), thin_piece(0, 0)
     square = (TILE, TILE)
     table = decay(jnp.abs(iota(square, 0) - iota(square, 1)))
     high, low = split(table)
@@ -252,6 +261,7 @@
     pl.semaphore_wait(near_in, 2)
     for dz in (-2, 2):
         signal(column_in, in_mem(dz, 0))
+    signal(other_in, in_mem(0, 1))
     a, b = remote(0)
     at_ref[...] = a.T
     for k in range(4):
@@ -272,9 +282,18 @@
             pkb[k * 32 + n : k * 32 + n + 8, :] = jnp.where(left, *picked)
 
     pl.semaphore_wait(column_in, 2)
-    signal(other_in, in_mem(0, 1))
-    for n, dz in enumerate(COLUMN):
-        send(pkb.at[piece_of(dz)], gat.at[n], sum_send, sum_recv, in_mem(dz, 0))
+    pl.semaphore_wait(other_in, 1)
+    signal(all_in, in_mem(0, 1))
+
+    @pl.when(core == 0)
+    def _():
+        for n, dz in enumerate(COLUMN):
+            send(pkb.at[wide_piece(dz)], gat.at[n], sum_send, sum_recv, in_mem(dz, 0))
+
+    @pl.when(core == 1)
+    def _():
+        for n, o in enumerate(WINDOW):
+            send(pkb.at[thin_piece(*o)], thin.at[n], sum_send, sum_recv, in_mem(*o))
 
     def find(k, carry):
         rows = pl.ds(pl.multiple_of((k // 2) * 128, 128), 128)
@@ -308,13 +327,26 @@
     loads[7].wait()
     valp[...] = pack(val) * (1.0 / saturation)
     wgtp[...] = pack(wgt) * (saturation * pair_scale())
-    pl.semaphore_wait(other_in, 1)
-    arrived(gat, sum_recv)
-    tot[...] = pkb[own, :] + jnp.sum(gat[...], axis=0)
-    for dz, dx in BACK:
-        send(tot, res.at[half, own], back_send, back_recv, in_mem(dz * mirror, dx))
-    res[half, own, :] = tot[...]
-    arrived(gat, back_recv)
+    pl.semaphore_wait(all_in, 1)
+
+    @pl.when(core == 0)
+    def _():
+        arrived(gat, sum_recv)
+        tot[...] = pkb[wide_own, :] + jnp.sum(gat[...], axis=0)
+        for o in WINDOW:
+            send(tot, res.at[half, wide_own], back_send, back_recv, in_mem(*o))
+        res[half, wide_own, :] = tot[...]
+        arrived(gat, back_recv)
+
+    @pl.when(core == 1)
+    def _():
+        arrived(thin.at[pl.ds(0, len(WINDOW))], sum_recv)
+        some = tot.at[pl.ds(0, THIN)]
+        some[...] = pkb[thin_own, :] + jnp.sum(thin[0 : len(WINDOW)], axis=0)
+        for o in AROUND:
+            send(some, res.at[turned, thin_own], back_send, back_recv, in_mem(*o))
+        res[turned, thin_own, :] = some[...]
+        arrived(thin, back_recv)
 
     total = res[0] + res[1]
     residual = wgtp[...] * jnp.tanh(total * (pair_scale() / saturation) - valp[...])
@@ -339,8 +371,16 @@
     share(1)
     for m in range(2):
         field[m] = ctl[m] + local(m)
-    arrived(gat, sum_send)
-    arrived(gat, back_send)
+    @pl.when(core == 0)
+    def _():
+        arrived(gat, sum_send)
+        arrived(gat, back_send)
+
+    @pl.when(core == 1)
+    def _():
+        arrived(thin.at[pl.ds(0, len(WINDOW))], sum_send)
+        arrived(thin, back_send)
+
     for turn in range(2):
         arrived(corners.at[turn], corner_send.at[turn])
         arrived(lines.at[turn], line_send.at[turn])
@@ -379,10 +419,10 @@
             vmem((2,) + square, f32), vmem(packed, i32), vmem(square, i32),
             vmem((LEVELS,) + packed, i32), vmem((TILE, 128), f32), vmem((TILE, 128), f32),
             vmem((2, 8, 384), f32), vmem((2, len(LINES), 8, 384), f32), vmem((2, len(CORNERS), 8, 128), f32),
-            vmem(packed, f32), vmem((len(COLUMN), ROWS, 128), f32), vmem((ROWS, 128), f32), vmem((2,) + packed, f32),
+            vmem(packed, f32), vmem((len(COLUMN), WIDE, 128), f32), vmem((len(AROUND), THIN, 128), f32), vmem((WIDE, 128), f32), vmem((2,) + packed, f32),
             vmem(packed, f32), vmem(packed, f32), vmem((TILE, 32), bf16),
             dma((8,)), dma((2,)), dma((2,)), dma((2,)), dma((2,)), dma, dma, dma, dma,
-            pltpu.SemaphoreType.REGULAR, pltpu.SemaphoreType.REGULAR, pltpu.SemaphoreType.REGULAR,
+            pltpu.SemaphoreType.REGULAR, pltpu.SemaphoreType.REGULAR, pltpu.SemaphoreType.REGULAR, pltpu.SemaphoreType.REGULAR,
         ],
         compiler_params=pltpu.CompilerParams(
             collective_id=0, has_side_effects=True, vmem_limit_bytes=24 << 20

time: 40.7 us -> 39.5 us (0.971)
  Pallas kernels: 40.5 us -> 39.3 us
    pallas_call x1, Pallas kernels: 39.4 us -> 38.2 us  [on_device(): pl.pallas_call(kernel, out_shape=[vmem((2,) + square, f32), vmem((32, TIL...]
where the time goes in v6:
time: 39.5 us; the launch traced here: 39.3 us
  Pallas kernels  39.3 us (99%)
    pallas_call x1, Pallas kernels, on_device(): pl.pallas_call(kernel, out_shape=[vmem((2,) + square, f32), vmem((32, TIL...  38.2 us
    pallas_call x1, Pallas kernels, on_device(): pl.pallas_call(join, out_shape=jax.ShapeDtypeStruct((2,) + square, f32),...  1.08 us

profile of v6, /device:TPU:1, one launch (start us, length us, event | category | flops | bytes accessed | tf_op | source)
XLA Modules:
  0.0 39.3 jit_solution(16726657119063767292)
XLA Ops:
  0.0 38.2 %shard_map.55 = (f32[2,256,256]{2,1,0:T(8,128)S(1)}, bf16[32,256]{1,0:T(8,128)(2,1)S(1)}, bf16[32,512]{1,0:T(8,128)(2,1)S(1)}) custom-call(f32[2,256,256]{2,1,0:T(8,128)} %control.1, bf16[2,256,256]{2,1,0:T(8,128)(2,1)} %ensemble.1, s32[64,256]{1,0:T(8,128)} %bitcast.3, f32[64,256]{1,0:T(8,128)} %bitcast.4, f32[64,256]{1,0:T(8,128)} %bitcast.5), custom_call_target="tpu_custom_call" | custom-call | tf_op jit(solution)/shard_map/pallas_call | solution.py:410
  38.2 1.1 %shard_map.56 = f32[2,256,256]{2,1,0:T(8,128)} custom-call(f32[2,256,256]{2,1,0:T(8,128)S(1)} %get-tuple-element.8.field, bf16[32,256]{1,0:T(8,128)(2,1)S(1)} %get-tuple-element.9.side_a, bf16[32,512]{1,0:T(8,128)(2,1)S(1)} %get-tuple-element.10.side_b), custom_call_target="tpu_custom_call" | custom-call | tf_op jit(solution)/shard_map/pallas_call | solution.py:434

commit v7 on v6

--- a/solution.py
+++ b/solution.py
@@ -107,7 +107,7 @@
 
 def kernel(
     control, ensemble, obs_index, obs_value, obs_weight, field, side_a, side_b,
-    ctl, ens, idx, val, wgt, thi, tlo, vhi, vlo, w0, idxp, first, nexts, fcol, bcol,
+    ctl, ens, idx, val, wgt, thi, tlo, vhi, vlo, w0, idxp, perm, first, nexts, fcol, bcol,
     msg, lines, corners, pkb, gat, thin, tot, res, valp, wgtp, at_ref,
     load_sem, line_send, line_recv, corner_send, corner_recv, sum_send, sum_recv, back_send, back_recv,
     near_in, column_in, other_in, all_in,
@@ -171,24 +171,30 @@
     def summarize(turn, over_x):
         x = 0.0
         for m in range(2):
-            y = fold(dot(ends16, vhi[m], 1, 1) + dot(ends16, vlo[m], 1, 1))
-            x = jnp.where((row >> 1) == 2 + m, y, x)
             for end in range(2):
                 line = jnp.concatenate([over_x[m][side][end] for side in range(2)], axis=1)
                 x = jnp.where(row == 2 * m + end, jnp.sum(line, axis=0, keepdims=True), x)
+        corner_f = jnp.sum(x * f_row, axis=1, keepdims=True)
+        corner_b = jnp.sum(x * b_row, axis=1, keepdims=True)
+        msg[turn, :, TILE:] = jnp.where(left, corner_f, corner_b)
+        return x
+
+    def complete(turn, x):
+        for m in range(2):
+            y = fold(dot(ends16, vhi[m], 1, 1) + dot(ends16, vlo[m], 1, 1))
+            x = jnp.where((row >> 1) == 2 + m, y, x)
         x_hi = x.astype(bf16).astype(f32)
         x16 = jnp.concatenate([x_hi, x - x_hi], axis=0).astype(bf16)
-        corner_f = jnp.sum(x * f_row, axis=1, keepdims=True)
-        corner_b = jnp.sum(x * b_row, axis=1, keepdims=True)
         msg[turn, :, 0:TILE] = fold(dot(x16, thi[...]) + dot(x16, tlo[...]))
-        msg[turn, :, TILE:] = jnp.where(left, corner_f, corner_b)
-
-    def share(turn):
+
+    def share_corners(turn):
         for n, o in enumerate(CORNERS):
             send(
                 msg.at[turn, :, pl.ds(TILE, 128)], corners.at[turn, n],
                 corner_send.at[turn], corner_recv.at[turn], in_plane(*o),
             )
+
+    def share_lines(turn):
         for n, o in enumerate(LINES):
             send(msg.at[turn], lines.at[turn, n], line_send.at[turn], line_recv.at[turn], in_plane(*o))
 
@@ -248,15 +254,38 @@
             vlo[m, rows, :] = low
             for side, lanes in enumerate(HALVES):
                 add_sums(m, side, ctl[m, rows, lanes], rows)
-    summarize(0, over_x)
+    complete(0, summarize(0, over_x))
     pl.semaphore_wait(barrier, len(peers))
     for dz in (-3, 3):
         signal(near_in, in_mem(dz, 0))
-    share(0)
+    share_corners(0)
+    share_lines(0)
     for m in range(2):
         w0[m] = local(m)
     loads[4].wait()
-    idxp[...] = pack(idx)
+    level = iota(narrow, 0)
+    order = []
+    for side in range(2):
+        at = [idx[8 * t : 8 * t + 8, side * 128 : side * 128 + 128] for t in range(8)]
+        rank = [jnp.zeros(narrow, i32) for t in range(8)]
+        for j in range(OBS):
+            here = at[j // 8][j % 8 : j % 8 + 1]
+            for t in range(8):
+                if t < j // 8:
+                    ahead = here < at[t]
+                elif t > j // 8:
+                    ahead = here <= at[t]
+                else:
+                    ahead = (here < at[t]) | ((here == at[t]) & (level > j % 8))
+                rank[t] = rank[t] + jnp.where(ahead, 1, 0)
+        found = [jnp.zeros(narrow, i32) for t in range(8)]
+        for j in range(OBS):
+            place_of = rank[j // 8][j % 8 : j % 8 + 1]
+            for t in range(8):
+                found[t] = jnp.where(place_of == level + 8 * t, side * OBS + j, found[t])
+        order += found
+    perm[...] = jnp.concatenate(order, axis=0).T
+    idxp[...] = take(pack(idx), perm[...])
     loads[5].wait()
     pl.semaphore_wait(near_in, 2)
     for dz in (-2, 2):
@@ -295,6 +324,10 @@
         for n, o in enumerate(WINDOW):
             send(pkb.at[thin_piece(*o)], thin.at[n], sum_send, sum_recv, in_mem(*o))
 
+    cells = idxp[...].T
+    for side in range(2):
+        idx[:, side * 128 : side * 128 + 128] = cells[side * OBS : side * OBS + OBS]
+
     def find(k, carry):
         rows = pl.ds(pl.multiple_of((k // 2) * 128, 128), 128)
         lanes = pl.ds(pl.multiple_of((k % 2) * 128, 128), 128)
@@ -306,27 +339,13 @@
         return carry
 
     lax.fori_loop(0, 4, find, 0)
-    level = iota(narrow, 0)
-    link = []
-    for side in range(2):
-        at = [idx[8 * t : 8 * t + 8, side * 128 : side * 128 + 128] for t in range(8)]
-        found = [jnp.full(narrow, -1, i32) for t in range(8)]
-        for j in range(OBS):
-            here = at[j // 8][j % 8 : j % 8 + 1]
-            for t in range(j // 8, 8):
-                hit = at[t] == here
-                if t == j // 8:
-                    hit = hit & (level > j % 8)
-                found[t] = jnp.where(hit, side * OBS + j, found[t])
-        link += found
-    link = jnp.concatenate(link, axis=0).T
+    cells = idxp[...] + jnp.where(iota((128, 128), 1) < OBS, 0, TILE)
     for n in range(LEVELS):
-        nexts[n] = link
-        link = jnp.where(link >= 0, take(link, jnp.maximum(link, 0)), -1)
+        nexts[n] = jnp.where(cells == pltpu.roll(cells, 1 << n, 1), 1.0, 0.0)
     loads[6].wait()
     loads[7].wait()
-    valp[...] = pack(val) * (1.0 / saturation)
-    wgtp[...] = pack(wgt) * (saturation * pair_scale())
+    valp[...] = take(pack(val), perm[...]) * (1.0 / saturation)
+    wgtp[...] = take(pack(wgt), perm[...]) * (saturation * pair_scale())
     pl.semaphore_wait(all_in, 1)
 
     @pl.when(core == 0)
@@ -351,8 +370,7 @@
     total = res[0] + res[1]
     residual = wgtp[...] * jnp.tanh(total * (pair_scale() / saturation) - valp[...])
     for n in range(LEVELS):
-        link = nexts[n]
-        residual = residual + jnp.where(link >= 0, take(residual, jnp.maximum(link, 0)), 0.0)
+        residual = residual + nexts[n] * pltpu.roll(residual, 1 << n, 1)
     over_x = [[[0.0, 0.0] for side in range(2)] for m in range(2)]
     for k in range(8):
         given = residual[k * 16 : k * 16 + 16]
@@ -367,8 +385,10 @@
                     vhi[m, rows, lanes] = high
                     vlo[m, rows, lanes] = low
                     over_x[m][side] = [old + new for old, new in zip(over_x[m][side], line_sums(v, rows))]
-    summarize(1, over_x)
-    share(1)
+    x = summarize(1, over_x)
+    share_corners(1)
+    complete(1, x)
+    share_lines(1)
     for m in range(2):
         field[m] = ctl[m] + local(m)
     @pl.when(core == 0)
@@ -416,8 +436,8 @@
             vmem((2,) + square, f32), vmem((2,) + square, bf16),
             vmem((OBS, TILE), i32), vmem((OBS, TILE), f32), vmem((OBS, TILE), f32),
             vmem(square, bf16), vmem(square, bf16), vmem((2,) + square, bf16), vmem((2,) + square, bf16),
-            vmem((2,) + square, f32), vmem(packed, i32), vmem(square, i32),
-            vmem((LEVELS,) + packed, i32), vmem((TILE, 128), f32), vmem((TILE, 128), f32),
+            vmem((2,) + square, f32), vmem(packed, i32), vmem(packed, i32), vmem(square, i32),
+            vmem((LEVELS,) + packed, f32), vmem((TILE, 128), f32), vmem((TILE, 128), f32),
             vmem((2, 8, 384), f32), vmem((2, len(LINES), 8, 384), f32), vmem((2, len(CORNERS), 8, 128), f32),
             vmem(packed, f32), vmem((len(COLUMN), WIDE, 128), f32), vmem((len(AROUND), THIN, 128), f32), vmem((WIDE, 128), f32), vmem((2,) + packed, f32),
             vmem(packed, f32), vmem(packed, f32), vmem((TILE, 32), bf16),

time: 39.5 us -> 39 us (0.987)
  Pallas kernels: 39.3 us -> 38.9 us
    pallas_call x1, Pallas kernels: 38.2 us -> 37.8 us  [on_device(): pl.pallas_call(kernel, out_shape=[vmem((2,) + square, f32), vmem((32, TIL...]
where the time goes in v7:
time: 39 us; the launch traced here: 38.9 us
  Pallas kernels  38.9 us (100%)
    pallas_call x1, Pallas kernels, on_device(): pl.pallas_call(kernel, out_shape=[vmem((2,) + square, f32), vmem((32, TIL...  37.8 us
    pallas_call x1, Pallas kernels, on_device(): pl.pallas_call(join, out_shape=jax.ShapeDtypeStruct((2,) + square, f32),...  1.08 us

profile of v7, /device:TPU:1, one launch (start us, length us, event | category | flops | bytes accessed | tf_op | source)
XLA Modules:
  0.0 38.9 jit_solution(10034865053343705792)
XLA Ops:
  0.0 37.8 %shard_map.55 = (f32[2,256,256]{2,1,0:T(8,128)S(1)}, bf16[32,256]{1,0:T(8,128)(2,1)S(1)}, bf16[32,512]{1,0:T(8,128)(2,1)S(1)}) custom-call(f32[2,256,256]{2,1,0:T(8,128)} %control.1, bf16[2,256,256]{2,1,0:T(8,128)(2,1)} %ensemble.1, s32[64,256]{1,0:T(8,128)} %bitcast.3, f32[64,256]{1,0:T(8,128)} %bitcast.4, f32[64,256]{1,0:T(8,128)} %bitcast.5), custom_call_target="tpu_custom_call" | custom-call | tf_op jit(solution)/shard_map/pallas_call | solution.py:430
  37.8 1.1 %shard_map.56 = f32[2,256,256]{2,1,0:T(8,128)} custom-call(f32[2,256,256]{2,1,0:T(8,128)S(1)} %get-tuple-element.8.field, bf16[32,256]{1,0:T(8,128)(2,1)S(1)} %get-tuple-element.9.side_a, bf16[32,512]{1,0:T(8,128)(2,1)S(1)} %get-tuple-element.10.side_b), custom_call_target="tpu_custom_call" | custom-call | tf_op jit(solution)/shard_map/pallas_call | solution.py:454

commit v8 on v7

--- a/solution.py
+++ b/solution.py
@@ -108,9 +108,9 @@
 def kernel(
     control, ensemble, obs_index, obs_value, obs_weight, field, side_a, side_b,
     ctl, ens, idx, val, wgt, thi, tlo, vhi, vlo, w0, idxp, perm, first, nexts, fcol, bcol,
-    msg, lines, corners, pkb, gat, thin, tot, res, valp, wgtp, at_ref,
+    msg, lines, corners, pkb, gat, thin, tot, some, res, valp, wgtp, at_ref,
     load_sem, line_send, line_recv, corner_send, corner_recv, sum_send, sum_recv, back_send, back_recv,
-    near_in, column_in, other_in, all_in,
+    wide_send, wide_recv, near_in, column_in, other_in, all_in, sibling_in,
 ):
     loads = [
         pltpu.make_async_copy(control.at[m, rows, :], ctl.at[m, rows, :], load_sem.at[2 * m + n])
@@ -133,7 +133,9 @@
 
     for peer in peers:
         signal(barrier, peer)
-    core = lax.rem(lax.axis_index("gx"), 2)
+    gx = lax.axis_index("gx")
+    core = lax.rem(gx, 2)
+    sibling = {"gx": gx + 1 - 2 * core}
     mem = lax.axis_index("mem")
     half, turned = mem // RING, lax.rem(mem, RING) // PIECES
 
@@ -313,11 +315,13 @@
     pl.semaphore_wait(column_in, 2)
     pl.semaphore_wait(other_in, 1)
     signal(all_in, in_mem(0, 1))
+    signal(sibling_in, sibling)
 
     @pl.when(core == 0)
     def _():
-        for n, dz in enumerate(COLUMN):
-            send(pkb.at[wide_piece(dz)], gat.at[n], sum_send, sum_recv, in_mem(dz, 0))
+        pl.semaphore_wait(sibling_in, 1)
+        for n, dz in enumerate(COLUMN + [0]):
+            send(pkb.at[wide_piece(dz)], gat.at[n], sum_send, wide_recv, in_mem(dz, 0) | sibling)
 
     @pl.when(core == 1)
     def _():
@@ -348,24 +352,23 @@
     wgtp[...] = take(pack(wgt), perm[...]) * (saturation * pair_scale())
     pl.semaphore_wait(all_in, 1)
 
-    @pl.when(core == 0)
-    def _():
-        arrived(gat, sum_recv)
-        tot[...] = pkb[wide_own, :] + jnp.sum(gat[...], axis=0)
-        for o in WINDOW:
-            send(tot, res.at[half, wide_own], back_send, back_recv, in_mem(*o))
-        res[half, wide_own, :] = tot[...]
-        arrived(gat, back_recv)
-
     @pl.when(core == 1)
     def _():
         arrived(thin.at[pl.ds(0, len(WINDOW))], sum_recv)
-        some = tot.at[pl.ds(0, THIN)]
         some[...] = pkb[thin_own, :] + jnp.sum(thin[0 : len(WINDOW)], axis=0)
         for o in AROUND:
             send(some, res.at[turned, thin_own], back_send, back_recv, in_mem(*o))
         res[turned, thin_own, :] = some[...]
+        pl.semaphore_wait(sibling_in, 1)
+        arrived(gat, wide_recv)
+        tot[...] = jnp.sum(gat[...], axis=0)
+        for o in WINDOW + [(0, 0)]:
+            send(tot, res.at[half, wide_own], wide_send, back_recv, in_mem(*o) | sibling)
         arrived(thin, back_recv)
+
+    @pl.when(core == 0)
+    def _():
+        arrived(res, back_recv)
 
     total = res[0] + res[1]
     residual = wgtp[...] * jnp.tanh(total * (pair_scale() / saturation) - valp[...])
@@ -394,12 +397,12 @@
     @pl.when(core == 0)
     def _():
         arrived(gat, sum_send)
-        arrived(gat, back_send)
 
     @pl.when(core == 1)
     def _():
         arrived(thin.at[pl.ds(0, len(WINDOW))], sum_send)
         arrived(thin, back_send)
+        arrived(gat, wide_send)
 
     for turn in range(2):
         arrived(corners.at[turn], corner_send.at[turn])
@@ -439,10 +442,10 @@
             vmem((2,) + square, f32), vmem(packed, i32), vmem(packed, i32), vmem(square, i32),
             vmem((LEVELS,) + packed, f32), vmem((TILE, 128), f32), vmem((TILE, 128), f32),
             vmem((2, 8, 384), f32), vmem((2, len(LINES), 8, 384), f32), vmem((2, len(CORNERS), 8, 128), f32),
-            vmem(packed, f32), vmem((len(COLUMN), WIDE, 128), f32), vmem((len(AROUND), THIN, 128), f32), vmem((WIDE, 128), f32), vmem((2,) + packed, f32),
+            vmem(packed, f32), vmem((RING, WIDE, 128), f32), vmem((len(AROUND), THIN, 128), f32), vmem((WIDE, 128), f32), vmem((THIN, 128), f32), vmem((2,) + packed, f32),
             vmem(packed, f32), vmem(packed, f32), vmem((TILE, 32), bf16),
-            dma((8,)), dma((2,)), dma((2,)), dma((2,)), dma((2,)), dma, dma, dma, dma,
-            pltpu.SemaphoreType.REGULAR, pltpu.SemaphoreType.REGULAR, pltpu.SemaphoreType.REGULAR, pltpu.SemaphoreType.REGULAR,
+            dma((8,)), dma((2,)), dma((2,)), dma((2,)), dma((2,)), dma, dma, dma, dma, dma, dma,
+            pltpu.SemaphoreType.REGULAR, pltpu.SemaphoreType.REGULAR, pltpu.SemaphoreType.REGULAR, pltpu.SemaphoreType.REGULAR, pltpu.SemaphoreType.REGULAR,
         ],
         compiler_params=pltpu.CompilerParams(
             collective_id=0, has_side_effects=True, vmem_limit_bytes=24 << 20

time: 39 us -> 38.3 us (0.982)
  Pallas kernels: 38.9 us -> 38.2 us
    pallas_call x1, Pallas kernels: 37.8 us -> 37.1 us  [on_device(): pl.pallas_call(kernel, out_shape=[vmem((2,) + square, f32), vmem((32, TIL...]
where the time goes in v8:
time: 38.3 us; the launch traced here: 38.2 us
  Pallas kernels  38.2 us (100%)
    pallas_call x1, Pallas kernels, on_device(): pl.pallas_call(kernel, out_shape=[vmem((2,) + square, f32), vmem((32, TIL...  37.1 us
    pallas_call x1, Pallas kernels, on_device(): pl.pallas_call(join, out_shape=jax.ShapeDtypeStruct((2,) + square, f32),...  1.08 us

profile of v8, /device:TPU:1, one launch (start us, length us, event | category | flops | bytes accessed | tf_op | source)
XLA Modules:
  0.0 38.2 jit_solution(9182921465604095161)
XLA Ops:
  0.0 37.1 %shard_map.55 = (f32[2,256,256]{2,1,0:T(8,128)S(1)}, bf16[32,256]{1,0:T(8,128)(2,1)S(1)}, bf16[32,512]{1,0:T(8,128)(2,1)S(1)}) custom-call(f32[2,256,256]{2,1,0:T(8,128)} %control.1, bf16[2,256,256]{2,1,0:T(8,128)(2,1)} %ensemble.1, s32[64,256]{1,0:T(8,128)} %bitcast.3, f32[64,256]{1,0:T(8,128)} %bitcast.4, f32[64,256]{1,0:T(8,128)} %bitcast.5), custom_call_target="tpu_custom_call" | custom-call | tf_op jit(solution)/shard_map/pallas_call | solution.py:433
  37.1 1.1 %shard_map.56 = f32[2,256,256]{2,1,0:T(8,128)} custom-call(f32[2,256,256]{2,1,0:T(8,128)S(1)} %get-tuple-element.8.field, bf16[32,256]{1,0:T(8,128)(2,1)S(1)} %get-tuple-element.9.side_a, bf16[32,512]{1,0:T(8,128)(2,1)S(1)} %get-tuple-element.10.side_b), custom_call_target="tpu_custom_call" | custom-call | tf_op jit(solution)/shard_map/pallas_call | solution.py:457

commit v9 on v8

--- a/solution.py
+++ b/solution.py
@@ -408,7 +408,7 @@
         arrived(corners.at[turn], corner_send.at[turn])
         arrived(lines.at[turn], line_send.at[turn])
     a, b = remote(1)
-    side_a[...] = a
+    side_a[...] = a.T
     side_b[...] = b
 
 
@@ -416,7 +416,7 @@
     copies = []
     for quarter in range(4):
         rows = slice(quarter * 64, quarter * 64 + 64)
-        update = dot(side_a[:, rows], side_b[...], 0, 0)
+        update = dot(side_a[rows, :], side_b[...])
         for m in range(2):
             both[m, rows, :] = field[m, rows, :] + update[:, m * TILE : (m + 1) * TILE]
             copy = pltpu.make_async_copy(both.at[m, rows, :], out.at[m, rows, :], sem.at[quarter, m])
@@ -432,7 +432,7 @@
     packed = (128, 128)
     field, side_a, side_b = pl.pallas_call(
         kernel,
-        out_shape=[vmem((2,) + square, f32), vmem((32, TILE), bf16), vmem((32, 2 * TILE), bf16)],
+        out_shape=[vmem((2,) + square, f32), vmem((TILE, 32), bf16), vmem((32, 2 * TILE), bf16)],
         in_specs=[pl.BlockSpec(memory_space=pltpu.HBM)] * 5,
         out_specs=[pl.BlockSpec(memory_space=vmem)] * 3,
         scratch_shapes=[

time: 38.3 us -> 38.2 us (level)
  no operation moved by 1% of the time
where the time goes in v9:
time: 38.2 us; the launch traced here: 38.1 us
  Pallas kernels  38.1 us (100%)
    pallas_call x1, Pallas kernels, on_device(): pl.pallas_call(kernel, out_shape=[vmem((2,) + square, f32), vmem((TILE, 3...  37.1 us
    pallas_call x1, Pallas kernels, on_device(): pl.pallas_call(join, out_shape=jax.ShapeDtypeStruct((2,) + square, f32),...  0.98 us

profile of v9, /device:TPU:1, one launch (start us, length us, event | category | flops | bytes accessed | tf_op | source)
XLA Modules:
  0.0 38.1 jit_solution(12172161739991299769)
XLA Ops:
  0.0 37.1 %shard_map.55 = (f32[2,256,256]{2,1,0:T(8,128)S(1)}, bf16[256,32]{1,0:T(8,128)(2,1)S(1)}, bf16[32,512]{1,0:T(8,128)(2,1)S(1)}) custom-call(f32[2,256,256]{2,1,0:T(8,128)} %control.1, bf16[2,256,256]{2,1,0:T(8,128)(2,1)} %ensemble.1, s32[64,256]{1,0:T(8,128)} %bitcast.3, f32[64,256]{1,0:T(8,128)} %bitcast.4, f32[64,256]{1,0:T(8,128)} %bitcast.5), custom_call_target="tpu_custom_call" | custom-call | tf_op jit(solution)/shard_map/pallas_call | solution.py:433
  37.1 1.0 %shard_map.56 = f32[2,256,256]{2,1,0:T(8,128)} custom-call(f32[2,256,256]{2,1,0:T(8,128)S(1)} %get-tuple-element.8.field, bf16[256,32]{1,0:T(8,128)(2,1)S(1)} %get-tuple-element.9.side_a, bf16[32,512]{1,0:T(8,128)(2,1)S(1)} %get-tuple-element.10.side_b), custom_call_target="tpu_custom_call" | custom-call | tf_op jit(solution)/shard_map/pallas_call | solution.py:457
